TPU v7x, 32 devices: a whole 2x2x4 slice. The times are simulated.
32 devices in a mesh: dp: 4 (over y, core), row: 2 (over x), col: 4 (over z).
Axes of the slice: x: 2, y: 2, z: 4, core: 2. Of those that a mesh axis runs over, the one named last changes fastest.
Arguments:
- x_in: bfloat16 [8192, 1024], P(('dp', 'row', 'col')), may hold values from -6 to 6
- ln1_gain: bfloat16 [2, 1024], P(None, ('dp', 'row')), may hold values from 0.25 to 1.75
- ln1_bias: bfloat16 [2, 1024], P(None, ('dp', 'row')), may hold values from -3 to 3
- w_qkv: bfloat16 [2, 1024, 3072], P(None, ('dp', 'row'), 'col'), may hold values from -0.7 to 0.7
- b_qv: bfloat16 [2, 2048], P(None, 'col'), may hold values from -3 to 3
- w_out: bfloat16 [2, 1024, 1024], P(None, 'col', ('dp', 'row')), may hold values from -0.5 to 0.5
- b_out: bfloat16 [2, 1024], P(None, ('dp', 'row')), may hold values from -3 to 3
- ln2_gain: bfloat16 [2, 1024], P(None, ('dp', 'row')), may hold values from 0.25 to 1.75
- ln2_bias: bfloat16 [2, 1024], P(None, ('dp', 'row')), may hold values from -3 to 3
- w_up: bfloat16 [2, 1024, 4096], P(None, ('dp', 'row'), 'col'), may hold values from -0.1875 to 0.1875
- b_up: bfloat16 [2, 4096], P(None, 'col'), may hold values from -3 to 3
- w_down: bfloat16 [2, 4096, 1024], P(None, 'col', ('dp', 'row')), may hold values from -0.09375 to 0.09375
- b_down: bfloat16 [2, 1024], P(None, ('dp', 'row')), may hold values from -3 to 3
- cotangent: bfloat16 [8192, 1024], P(('dp', 'row', 'col')), may hold values from -6 to 6
Outputs:
- out_stream: bfloat16 [8192, 1024], P(('dp', 'row', 'col'))
- grad_in: float32 [8192, 1024], P(('dp', 'row', 'col'))
- ln1_gain_grad: float32 [2, 1024], P(None, ('dp', 'row'))
- ln1_bias_grad: float32 [2, 1024], P(None, ('dp', 'row'))
- w_qkv_grad: float32 [2, 1024, 3072], P(None, ('dp', 'row'), 'col')
- b_qv_grad: float32 [2, 2048], P(None, 'col')
- w_out_grad: float32 [2, 1024, 1024], P(None, 'col', ('dp', 'row'))
- b_out_grad: float32 [2, 1024], P(None, ('dp', 'row'))
- ln2_gain_grad: float32 [2, 1024], P(None, ('dp', 'row'))
- ln2_bias_grad: float32 [2, 1024], P(None, ('dp', 'row'))
- w_up_grad: float32 [2, 1024, 4096], P(None, ('dp', 'row'), 'col')
- b_up_grad: float32 [2, 4096], P(None, 'col')
- w_down_grad: float32 [2, 4096, 1024], P(None, 'col', ('dp', 'row'))
- b_down_grad: float32 [2, 1024], P(None, ('dp', 'row'))
All inputs are finite; a program needn't handle non-finite values.
Results may differ from a plain program's by a relative error of at most 0.04.
Values may be sent and summed in bfloat16 or wider, within the bound.
No kernel may reach another device: no remote copies, remote signals or barrier semaphores. Data moves between devices by JAX's collectives and lax.ppermute only.
A program may use at most 192 MiB of HBM per device.

v0:
```python
import jax
import jax.numpy as jnp
from jax import lax
from jax.sharding import PartitionSpec as P

HEADS = 16
HEAD_DIM = 64
SEQ = 1024
LAYERS = 2


epsilon = 1e-05
gelu_scale = 0.7978845608028654
gelu_cube = 0.044715


def layer_norm_parts(values, gain_vec, offset_vec):
    center = jnp.mean(values, axis=-1, keepdims=True)
    centered = values - center
    spread = jnp.mean(centered * centered, axis=-1, keepdims=True)
    inverse = lax.rsqrt(spread + epsilon)
    normal = centered * inverse
    return (normal * gain_vec + offset_vec, normal, inverse)


def norm_backward(upstream, normal, inverse, gain_vec):
    scaled = upstream * gain_vec
    mean_first = jnp.mean(scaled, axis=-1, keepdims=True)
    second = jnp.mean(scaled * normal, axis=-1, keepdims=True)
    return inverse * (scaled - mean_first - normal * second)


def gelu_parts(pre_act):
    tangent = jnp.tanh(gelu_scale * (pre_act + gelu_cube * pre_act * pre_act * pre_act))
    result = 0.5 * pre_act * (1.0 + tangent)
    derivative = 0.5 * (1.0 + tangent) + 0.5 * pre_act * (1.0 - tangent * tangent) * gelu_scale * (
        1.0 + 3.0 * gelu_cube * pre_act * pre_act
    )
    return (result, derivative)


def head_slopes(local_heads):
    total_heads = local_heads * lax.axis_size("col")
    head_order = (
        lax.axis_index("col") * local_heads + jnp.arange(local_heads, dtype=jnp.int32)
    ).astype(jnp.float32)
    return jnp.exp2(-8.0 * (head_order + 1.0) / total_heads)


def block_scores(queries, keys_seq, slopes, row_first):
    scores = jnp.einsum(
        "qhd,khd->hqk", queries, keys_seq, preferred_element_type=jnp.float32
    ) * queries.shape[-1] ** (-0.5)
    row_ids = row_first + jnp.arange(queries.shape[0], dtype=jnp.int32)
    key_ids = jnp.arange(keys_seq.shape[0], dtype=jnp.int32)
    offset = (key_ids[None, :] - row_ids[:, None]).astype(jnp.float32)
    scores = scores + slopes[:, None, None] * offset[None]
    return jnp.where((key_ids[None, :] <= row_ids[:, None])[None], scores, -1e30)


def attend_sequence(packed_seq, slopes, block_rows):
    keys_seq = packed_seq[:, :, 1]
    values_seq = packed_seq[:, :, 2]
    out_blocks = []
    log_blocks = []
    for block_index in range(packed_seq.shape[0] // block_rows):
        row_first = block_index * block_rows
        scores = block_scores(
            packed_seq[row_first : row_first + block_rows, :, 0], keys_seq, slopes, row_first
        )
        peak = jnp.max(scores, axis=-1, keepdims=True)
        powers = jnp.exp(scores - peak)
        row_total = jnp.sum(powers, axis=-1, keepdims=True)
        weights = (powers / row_total).astype(jnp.bfloat16)
        mixed_rows = jnp.einsum(
            "hqk,khd->qhd", weights, values_seq, preferred_element_type=jnp.float32
        )
        out_blocks.append(mixed_rows.astype(jnp.bfloat16))
        log_blocks.append((peak + jnp.log(row_total))[..., 0])
    return (jnp.concatenate(out_blocks, axis=0), jnp.concatenate(log_blocks, axis=1))


def attend_backward(packed_seq, log_seq, grad_seq, slopes, block_rows):
    keys_seq = packed_seq[:, :, 1]
    values_seq = packed_seq[:, :, 2]
    scale = packed_seq.shape[-1] ** (-0.5)
    key_grad = jnp.zeros(keys_seq.shape, jnp.float32)
    value_grad = jnp.zeros(values_seq.shape, jnp.float32)
    query_blocks = []
    for block_index in range(packed_seq.shape[0] // block_rows):
        row_first = block_index * block_rows
        queries = packed_seq[row_first : row_first + block_rows, :, 0]
        scores = block_scores(queries, keys_seq, slopes, row_first)
        probs = jnp.exp(scores - log_seq[:, row_first : row_first + block_rows, None])
        grad_block = grad_seq[row_first : row_first + block_rows]
        prob_grad = jnp.einsum(
            "qhd,khd->hqk", grad_block, values_seq, preferred_element_type=jnp.float32
        )
        inner_sum = jnp.sum(probs * prob_grad, axis=-1, keepdims=True)
        score_grad = (probs * (prob_grad - inner_sum)).astype(jnp.bfloat16)
        query_blocks.append(
            jnp.einsum("hqk,khd->qhd", score_grad, keys_seq, preferred_element_type=jnp.float32)
            * scale
        )
        key_grad = (
            key_grad
            + jnp.einsum("hqk,qhd->khd", score_grad, queries, preferred_element_type=jnp.float32)
            * scale
        )
        value_grad = value_grad + jnp.einsum(
            "hqk,qhd->khd",
            probs.astype(jnp.bfloat16),
            grad_block,
            preferred_element_type=jnp.float32,
        )
    return jnp.stack([jnp.concatenate(query_blocks, axis=0), key_grad, value_grad], axis=2)


def gather_weights(tables, layer_index):
    gain_one, bias_one, qkv_w, out_w, gain_two, bias_two, up_w, down_w, out_b, down_b = tables
    return (
        lax.all_gather(gain_one[layer_index], ("dp", "row"), axis=0, tiled=True),
        lax.all_gather(bias_one[layer_index], ("dp", "row"), axis=0, tiled=True),
        lax.all_gather(qkv_w[layer_index], ("dp", "row"), axis=0, tiled=True),
        lax.all_gather(out_w[layer_index], ("dp", "row"), axis=1, tiled=True),
        lax.all_gather(gain_two[layer_index], ("dp", "row"), axis=0, tiled=True),
        lax.all_gather(bias_two[layer_index], ("dp", "row"), axis=0, tiled=True),
        lax.all_gather(up_w[layer_index], ("dp", "row"), axis=0, tiled=True),
        lax.all_gather(down_w[layer_index], ("dp", "row"), axis=1, tiled=True),
        lax.all_gather(out_b[layer_index], ("dp", "row"), axis=0, tiled=True),
        lax.all_gather(down_b[layer_index], ("dp", "row"), axis=0, tiled=True),
    )


def spread_rows(normed, weight, bias_vec):
    return (
        jnp.dot(
            lax.all_gather(normed, "col", axis=0, tiled=True),
            weight,
            preferred_element_type=jnp.float32,
        )
        + bias_vec
    )


def branch_rows(left, weight, row_count):
    return lax.psum_scatter(
        jnp.dot(
            lax.dynamic_slice_in_dim(left, jnp.int32(0), lax.axis_size("col") * row_count, 0),
            weight,
            preferred_element_type=jnp.float32,
        ).astype(jnp.bfloat16),
        "col",
        scatter_dimension=0,
        tiled=True,
    ).astype(jnp.float32)


def pull_rows(upstream, kept_left, weight):
    shard_rows = lax.all_gather(upstream, "col", axis=0, tiled=True)
    first_row = jnp.int32(0)
    weight_grad = jnp.zeros((kept_left.shape[1], weight.shape[1]), jnp.float32)
    row_grad = jnp.zeros((kept_left.shape[0], weight.shape[0]), jnp.float32)
    left_rows = lax.dynamic_slice_in_dim(kept_left, first_row, shard_rows.shape[0], 0)
    weight_grad = weight_grad + jnp.einsum(
        "nf,nd->fd", left_rows, shard_rows, preferred_element_type=jnp.float32
    )
    product = jnp.einsum("nd,fd->nf", shard_rows, weight, preferred_element_type=jnp.float32)
    row_grad = lax.dynamic_update_slice_in_dim(row_grad, product, first_row, 0)
    return (weight_grad, row_grad)


def left_grads(normed, upstream):
    start_state = jnp.zeros((normed.shape[1], upstream.shape[1]), jnp.float32)
    shard_rows = lax.all_gather(normed, "col", axis=0, tiled=True)
    right_rows = lax.dynamic_slice_in_dim(upstream, jnp.int32(0), shard_rows.shape[0], 0)
    return start_state + jnp.einsum(
        "nd,nf->df", shard_rows, right_rows, preferred_element_type=jnp.float32
    )


def input_rows(upstream, weight, row_count):
    return lax.psum_scatter(
        jnp.einsum(
            "nf,df->nd",
            lax.dynamic_slice_in_dim(upstream, jnp.int32(0), lax.axis_size("col") * row_count, 0),
            weight,
            preferred_element_type=jnp.float32,
        ).astype(jnp.bfloat16),
        "col",
        scatter_dimension=0,
        tiled=True,
    ).astype(jnp.float32)


def reduce_grads(qkv_grad, out_grad, up_grad, down_grad, vectors):
    return (
        lax.psum_scatter(
            qkv_grad.astype(jnp.bfloat16), ("dp", "row"), scatter_dimension=0, tiled=True
        ).astype(jnp.float32),
        lax.psum_scatter(
            out_grad.astype(jnp.bfloat16), ("dp", "row"), scatter_dimension=1, tiled=True
        ).astype(jnp.float32),
        lax.psum_scatter(
            up_grad.astype(jnp.bfloat16), ("dp", "row"), scatter_dimension=0, tiled=True
        ).astype(jnp.float32),
        lax.psum_scatter(
            down_grad.astype(jnp.bfloat16), ("dp", "row"), scatter_dimension=1, tiled=True
        ).astype(jnp.float32),
        lax.psum_scatter(
            vectors.astype(jnp.bfloat16), ("dp", "row"), scatter_dimension=1, tiled=True
        ).astype(jnp.float32),
    )


def local(
    x_in,
    ln1_gain,
    ln1_bias,
    w_qkv,
    b_qv,
    w_out,
    b_out,
    ln2_gain,
    ln2_bias,
    w_up,
    b_up,
    w_down,
    b_down,
    cotangent,
):
    local_heads = HEADS // lax.axis_size("col")
    block_rows = min(512, SEQ)
    slopes = head_slopes(local_heads)
    tables = (ln1_gain, ln1_bias, w_qkv, w_out, ln2_gain, ln2_bias, w_up, w_down, b_out, b_down)
    row_count = x_in.shape[0]
    stream = x_in.astype(jnp.float32)
    saved = []
    for layer_index in range(LAYERS):
        fetched = gather_weights(tables, layer_index)
        (
            gain_one,
            bias_one,
            qkv_full,
            out_full,
            gain_two,
            bias_two,
            up_full,
            down_full,
            out_bias,
            down_bias,
        ) = fetched
        normed_one, normal_one, inverse_one = layer_norm_parts(
            stream, gain_one.astype(jnp.float32), bias_one.astype(jnp.float32)
        )
        normed_one = normed_one.astype(jnp.bfloat16)
        pair = b_qv[layer_index].astype(jnp.float32).reshape(local_heads, 2, HEAD_DIM)
        merged = jnp.stack([pair[:, 0], jnp.zeros_like(pair[:, 0]), pair[:, 1]], axis=1).reshape(-1)
        packed = spread_rows(normed_one, qkv_full, merged).astype(jnp.bfloat16)
        grouped = packed.reshape(-1, SEQ, local_heads, 3, HEAD_DIM)
        mixed_seq, log_totals = lax.map(
            lambda packed_seq: attend_sequence(packed_seq, slopes, block_rows), grouped
        )
        mixed_rows = mixed_seq.reshape(packed.shape[0], local_heads * HEAD_DIM)
        middle = stream + (
            branch_rows(mixed_rows, out_full, row_count) + out_bias.astype(jnp.float32)
        )
        normed_two, normal_two, inverse_two = layer_norm_parts(
            middle, gain_two.astype(jnp.float32), bias_two.astype(jnp.float32)
        )
        normed_two = normed_two.astype(jnp.bfloat16)
        pre_act = spread_rows(normed_two, up_full, b_up[layer_index].astype(jnp.float32))
        activated = gelu_parts(pre_act)[0].astype(jnp.bfloat16)
        stream = middle + (
            branch_rows(activated, down_full, row_count) + down_bias.astype(jnp.float32)
        )
        kept_weights = fetched
        saved.append(
            (
                normal_one,
                inverse_one,
                normed_one,
                grouped,
                log_totals,
                mixed_rows,
                normal_two,
                inverse_two,
                normed_two,
                pre_act,
                activated,
                kept_weights,
            )
        )
    out_stream = stream.astype(jnp.bfloat16)
    upstream = cotangent.astype(jnp.float32)
    results = [None] * LAYERS
    for layer_index in reversed(range(LAYERS)):
        (
            normal_one,
            inverse_one,
            normed_one,
            grouped,
            log_totals,
            mixed_rows,
            normal_two,
            inverse_two,
            normed_two,
            pre_act,
            activated,
            kept_weights,
        ) = saved[layer_index]
        fetched = kept_weights
        (
            gain_one,
            bias_one,
            qkv_full,
            out_full,
            gain_two,
            bias_two,
            up_full,
            down_full,
            out_bias,
            down_bias,
        ) = fetched
        branch_grad = upstream.astype(jnp.bfloat16)
        down_bias_grad = jnp.sum(branch_grad.astype(jnp.float32), axis=0)
        down_grad, act_grad = pull_rows(branch_grad, activated, down_full)
        derivative = gelu_parts(pre_act)[1]
        pre_grad = (act_grad * derivative).astype(jnp.bfloat16)
        up_bias_grad = jnp.sum(pre_grad.astype(jnp.float32), axis=0)
        up_grad = left_grads(normed_two, pre_grad)
        normed_grad = input_rows(pre_grad, up_full, row_count)
        gain_two_grad = jnp.sum(normed_grad * normal_two, axis=0)
        bias_two_grad = jnp.sum(normed_grad, axis=0)
        middle_grad = upstream + norm_backward(
            normed_grad, normal_two, inverse_two, gain_two.astype(jnp.float32)
        )
        attn_grad = middle_grad.astype(jnp.bfloat16)
        out_bias_grad = jnp.sum(attn_grad.astype(jnp.float32), axis=0)
        out_grad, mixed_grad = pull_rows(attn_grad, mixed_rows, out_full)
        mixed_grad = mixed_grad.astype(jnp.bfloat16).reshape(
            grouped.shape[0], SEQ, local_heads, HEAD_DIM
        )
        packed_grad = lax.map(
            lambda inputs: attend_backward(inputs[0], inputs[1], inputs[2], slopes, block_rows),
            (grouped, log_totals, mixed_grad),
        )
        packed_grad = packed_grad.reshape(mixed_rows.shape[0], 3 * local_heads * HEAD_DIM).astype(
            jnp.bfloat16
        )
        column_sums = jnp.sum(packed_grad.astype(jnp.float32), axis=0).reshape(
            local_heads, 3, HEAD_DIM
        )
        qv_bias_grad = jnp.stack([column_sums[:, 0], column_sums[:, 2]], axis=1).reshape(-1)
        qkv_grad = left_grads(normed_one, packed_grad)
        first_grad = input_rows(packed_grad, qkv_full, row_count)
        gain_one_grad = jnp.sum(first_grad * normal_one, axis=0)
        bias_one_grad = jnp.sum(first_grad, axis=0)
        upstream = middle_grad + norm_backward(
            first_grad, normal_one, inverse_one, gain_one.astype(jnp.float32)
        )
        vectors = jnp.stack(
            [
                gain_one_grad,
                bias_one_grad,
                gain_two_grad,
                bias_two_grad,
                out_bias_grad,
                down_bias_grad,
            ]
        )
        qkv_share, out_share, up_share, down_share, vector_share = reduce_grads(
            qkv_grad, out_grad, up_grad, down_grad, vectors
        )
        vector_share = lax.psum(vector_share, "col")
        qv_share, up_bias_share = lax.psum((qv_bias_grad, up_bias_grad), ("dp", "row"))
        results[layer_index] = (
            vector_share,
            qkv_share,
            qv_share,
            out_share,
            up_share,
            up_bias_share,
            down_share,
        )

    def stacked(member):
        return jnp.stack([results[layer_index][member] for layer_index in range(LAYERS)])

    vector_rows = stacked(0)
    return (
        out_stream,
        upstream,
        vector_rows[:, 0],
        vector_rows[:, 1],
        stacked(1),
        stacked(2),
        stacked(3),
        vector_rows[:, 4],
        vector_rows[:, 2],
        vector_rows[:, 3],
        stacked(4),
        stacked(5),
        stacked(6),
        vector_rows[:, 5],
    )


def solution(mesh):
    return jax.shard_map(
        local,
        mesh=mesh,
        in_specs=(
            P(("dp", "row", "col"), None),
            P(None, ("dp", "row")),
            P(None, ("dp", "row")),
            P(None, ("dp", "row"), "col"),
            P(None, "col"),
            P(None, "col", ("dp", "row")),
            P(None, ("dp", "row")),
            P(None, ("dp", "row")),
            P(None, ("dp", "row")),
            P(None, ("dp", "row"), "col"),
            P(None, "col"),
            P(None, "col", ("dp", "row")),
            P(None, ("dp", "row")),
            P(("dp", "row", "col"), None),
        ),
        out_specs=(
            P(("dp", "row", "col"), None),
            P(("dp", "row", "col"), None),
            P(None, ("dp", "row")),
            P(None, ("dp", "row")),
            P(None, ("dp", "row"), "col"),
            P(None, "col"),
            P(None, "col", ("dp", "row")),
            P(None, ("dp", "row")),
            P(None, ("dp", "row")),
            P(None, ("dp", "row")),
            P(None, ("dp", "row"), "col"),
            P(None, "col"),
            P(None, "col", ("dp", "row")),
            P(None, ("dp", "row")),
        ),
        check_vma=False,
    )
```

profile of v0, /device:TPU:0, one launch (start us, length us, event | category | flops | bytes accessed | tf_op | source)
XLA Modules:
  0.0 1460.9 jit_solution(3829187963355352520)
XLA Ops:
  9.8 12.3 all-gather.1
  22.9 11.2 all-gather
  41.0 18.8 %all-gather.3 = bf16[1,256,1024]{2,1,0:T(8,128)(2,1)S(1)} all-gather(bf16[1,256,128]{2,1,0:T(8,128)(2,1)S(1)} %get-tuple-element.133), channel_id=5, replica_groups=mesh['dp'=4,'row'=2,'col'=4] {'dp','row'}, dimensions={2}, use_global_device_ids=true | all-gather | bytes 589824 | tf_op jit(solution)/shard_map/all_gather | solution.py:125
  63.0 23.6 %all-gather.35.cloned.1.call-done = bf16[1024,1024]{1,0:T(8,128)(2,1)} async-done(((bf16[256,1024]{1,0:T(8,128)(2,1)}), bf16[1024,1024]{1,0:T(8,128)(2,1)}) %all-gather.35.cloned.1.call-update) | async-done | bytes 2097168 | tf_op jit(solution)/shard_map/all_gather | solution.py:138
  110.6 11.1 all-gather.6
  121.8 11.5 all-gather.5
  133.3 11.5 all-gather.4
  144.8 7.4 reduce-scatter.31.cloned.1.call-done
  158.1 22.9 %all-gather.53.cloned.1.call-done = bf16[1,1024,1024]{2,1,0:T(8,128)(2,1)} async-done(((bf16[1,128,1024]{2,1,0:T(8,128)(2,1)}), bf16[1,1024,1024]{2,1,0:T(8,128)(2,1)}) %all-gather.53.cloned.1.call-update) | async-done | bytes 2097168 | tf_op jit(solution)/shard_map/all_gather | solution.py:128
  181.0 47.7 %all-gather.37.cloned.1.call-done = bf16[1024,1024]{1,0:T(8,128)(2,1)} async-done(((bf16[256,1024]{1,0:T(8,128)(2,1)}), bf16[1024,1024]{1,0:T(8,128)(2,1)}) %all-gather.37.cloned.1.call-update) | async-done | bytes 2097168 | tf_op jit(solution)/shard_map/all_gather | solution.py:138
  235.2 22.7 %all-gather.55.cloned.1.call-done = bf16[1,1024,1024]{2,1,0:T(8,128)(2,1)} async-done(((bf16[1,1024,128]{2,1,0:T(8,128)(2,1)}), bf16[1,1024,1024]{2,1,0:T(8,128)(2,1)}) %all-gather.55.cloned.1.call-update) | async-done | bytes 2097168 | tf_op jit(solution)/shard_map/all_gather | solution.py:129
  265.8 10.3 all-gather.11
  276.1 11.5 all-gather.10
  287.6 11.5 all-gather.9
  299.1 9.6 reduce-scatter.33.cloned.1.call-done
  311.6 17.8 %all-gather.13 = bf16[1,256,1024]{2,1,0:T(8,128)(2,1)S(1)} all-gather(bf16[1,256,128]{2,1,0:T(8,128)(2,1)S(1)} %get-tuple-element.132), channel_id=15, replica_groups=mesh['dp'=4,'row'=2,'col'=4] {'dp','row'}, dimensions={2}, use_global_device_ids=true | all-gather | bytes 589824 | tf_op jit(solution)/shard_map/all_gather | solution.py:125
  335.8 47.8 %all-gather.39.cloned.1.call-done = bf16[1024,1024]{1,0:T(8,128)(2,1)} async-done(((bf16[256,1024]{1,0:T(8,128)(2,1)}), bf16[1024,1024]{1,0:T(8,128)(2,1)}) %all-gather.39.cloned.1.call-update) | async-done | bytes 2097168 | tf_op jit(solution)/shard_map/all_gather | solution.py:138
  405.6 10.8 all-gather.16
  416.5 11.5 all-gather.15
  427.9 11.5 all-gather.14
  439.4 8.0 reduce-scatter.35.cloned.1.call-done
  451.4 25.5 %all-gather.59.cloned.1.call-done = bf16[1,1024,1024]{2,1,0:T(8,128)(2,1)} async-done(((bf16[1,128,1024]{2,1,0:T(8,128)(2,1)}), bf16[1,1024,1024]{2,1,0:T(8,128)(2,1)}) %all-gather.59.cloned.1.call-update) | async-done | bytes 2097168 | tf_op jit(solution)/shard_map/all_gather | solution.py:128
  476.9 47.7 %all-gather.41.cloned.1.call-done = bf16[1024,1024]{1,0:T(8,128)(2,1)} async-done(((bf16[256,1024]{1,0:T(8,128)(2,1)}), bf16[1024,1024]{1,0:T(8,128)(2,1)}) %all-gather.41.cloned.1.call-update) | async-done | bytes 2097168 | tf_op jit(solution)/shard_map/all_gather | solution.py:138
  531.1 39.6 %all-gather.43.cloned.1.call-done = bf16[1024,1024]{1,0:T(8,128)(2,1)} async-done(((bf16[256,1024]{1,0:T(8,128)(2,1)}), bf16[1024,1024]{1,0:T(8,128)(2,1)}) %all-gather.43.cloned.1.call-update) | async-done | bytes 2097168 | tf_op jit(solution)/shard_map/all_gather | solution.py:160
  570.7 29.2 %all-gather.61.cloned.1.call-done = bf16[1,1024,1024]{2,1,0:T(8,128)(2,1)} async-done(((bf16[1,1024,128]{2,1,0:T(8,128)(2,1)}), bf16[1,1024,1024]{2,1,0:T(8,128)(2,1)}) %all-gather.61.cloned.1.call-update) | async-done | bytes 2097168 | tf_op jit(solution)/shard_map/all_gather | solution.py:129
  599.9 8.7 convert_reduce_fusion
  620.8 10.8 all-gather.19
  631.5 25.9 %reduce-scatter.39.cloned.1.call-done = bf16[256,1024]{1,0:T(8,128)(2,1)} async-done(((bf16[1024,1024]{1,0:T(8,128)(2,1)}), bf16[256,1024]{1,0:T(8,128)(2,1)}) %reduce-scatter.39.cloned.1.call-update) | async-done | bytes 524304 | tf_op jit(solution)/shard_map/reduce_scatter | solution.py:183
  657.5 45.0 %reduce-scatter.37.cloned.1.call-done = bf16[256,1024]{1,0:T(8,128)(2,1)} async-done(((bf16[1024,1024]{1,0:T(8,128)(2,1)}), bf16[256,1024]{1,0:T(8,128)(2,1)}) %reduce-scatter.37.cloned.1.call-update) | async-done | bytes 524304 | tf_op jit(solution)/shard_map/reduce_scatter | solution.py:147
  708.6 44.7 %all-gather.45.cloned.1.call-done = bf16[1024,1024]{1,0:T(8,128)(2,1)} async-done(((bf16[256,1024]{1,0:T(8,128)(2,1)}), bf16[1024,1024]{1,0:T(8,128)(2,1)}) %all-gather.45.cloned.1.call-update) | async-done | bytes 2097168 | tf_op jit(solution)/shard_map/all_gather | solution.py:160
  755.9 7.8 multiply_reduce_fusion.3
  788.6 42.1 %reduce-scatter.41.cloned.1.call-done = bf16[256,1024]{1,0:T(8,128)(2,1)} async-done(((bf16[1024,1024]{1,0:T(8,128)(2,1)}), bf16[256,1024]{1,0:T(8,128)(2,1)}) %reduce-scatter.41.cloned.1.call-update) | async-done | bytes 524304 | tf_op jit(solution)/shard_map/reduce_scatter | solution.py:183
  835.3 44.9 %all-gather.47.cloned.1.call-done = bf16[1024,1024]{1,0:T(8,128)(2,1)} async-done(((bf16[256,1024]{1,0:T(8,128)(2,1)}), bf16[1024,1024]{1,0:T(8,128)(2,1)}) %all-gather.47.cloned.1.call-update) | async-done | bytes 2097168 | tf_op jit(solution)/shard_map/all_gather | solution.py:160
  880.2 8.0 convert_reduce_fusion.1
  893.3 42.5 %reduce-scatter.43.cloned.1.call-done = bf16[256,1024]{1,0:T(8,128)(2,1)} async-done(((bf16[1024,1024]{1,0:T(8,128)(2,1)}), bf16[256,1024]{1,0:T(8,128)(2,1)}) %reduce-scatter.43.cloned.1.call-update) | async-done | bytes 524304 | tf_op jit(solution)/shard_map/reduce_scatter | solution.py:183
  974.0 11.5 all-gather.49.cloned.1.call-done
  1033.8 32.8 %reduce-scatter.61.cloned.1.call-done = bf16[128,256]{1,0:T(8,128)(2,1)} async-done(((bf16[1024,256]{1,0:T(8,128)(2,1)}), bf16[128,256]{1,0:T(8,128)(2,1)}) %reduce-scatter.61.cloned.1.call-update) | async-done | bytes 65552
  1067.6 36.2 %reduce-scatter.57.cloned.1.call-done = bf16[128,6]{1,0:T(8,128)(2,1)} async-done(((bf16[1024,6]{1,0:T(8,128)(2,1)}), bf16[128,6]{1,0:T(8,128)(2,1)}) %reduce-scatter.57.cloned.1.call-update) | async-done | bytes 1552
  1104.6 43.6 %reduce-scatter.63.cloned.1.call-done = bf16[128,1024]{1,0:T(8,128)(2,1)} async-done(((bf16[1024,1024]{1,0:T(8,128)(2,1)}), bf16[128,1024]{1,0:T(8,128)(2,1)}) %reduce-scatter.63.cloned.1.call-update) | async-done | bytes 262160
  1149.3 43.2 %reduce-scatter.53.cloned.1.call-done = bf16[128,1024]{1,0:T(8,128)(2,1)} async-done(((bf16[1024,1024]{1,0:T(8,128)(2,1)}), bf16[128,1024]{1,0:T(8,128)(2,1)}) %reduce-scatter.53.cloned.1.call-update) | async-done | bytes 262160 | tf_op jit(solution)/shard_map/reduce_scatter | solution.py:204
  1192.5 44.3 %reduce-scatter.51.cloned.1.call-done = bf16[128,1024]{1,0:T(8,128)(2,1)} async-done(((bf16[1024,1024]{1,0:T(8,128)(2,1)}), bf16[128,1024]{1,0:T(8,128)(2,1)}) %reduce-scatter.51.cloned.1.call-update) | async-done | bytes 262160 | tf_op jit(solution)/shard_map/reduce_scatter | solution.py:204
  1240.0 23.8 %all-reduce = (f32[1,512]{1,0:T(1,128)S(1)}, f32[1,512]{1,0:T(1,128)S(1)}, f32[1,1024]{1,0:T(1,128)S(1)}, f32[1,1024]{1,0:T(1,128)S(1)}) all-reduce(f32[1,512]{1,0:T(1,128)S(1)} %stack.217, f32[1,512]{1,0:T(1,128)S(1)} %stack.215, f32[1,1024]{1,0:T(1,128)S(1)} %bitcast.360, ...), channel_id=1, replica_groups=mesh['dp'=4,'row'=2,'col'=4] {'dp','row'}, use_global_device_ids=true, to_apply=%region_57.58 | all-reduce | flops 3072 | bytes 24576 | tf_op jit(solution)/shard_map/psum | solution.py:376
  1265.0 9.6 reduce-scatter.59.cloned.1.call-done
  1276.3 40.0 %reduce-scatter.49.cloned.1.call-done = bf16[128,768]{1,0:T(8,128)(2,1)} async-done(((bf16[1024,768]{1,0:T(8,128)(2,1)}), bf16[128,768]{1,0:T(8,128)(2,1)}) %reduce-scatter.49.cloned.1.call-update) | async-done | bytes 196624 | tf_op jit(solution)/shard_map/reduce_scatter | solution.py:198
  1316.3 41.5 %reduce-scatter.47.cloned.1.call-done = bf16[128,768]{1,0:T(8,128)(2,1)} async-done(((bf16[1024,768]{1,0:T(8,128)(2,1)}), bf16[128,768]{1,0:T(8,128)(2,1)}) %reduce-scatter.47.cloned.1.call-update) | async-done | bytes 196624 | tf_op jit(solution)/shard_map/reduce_scatter | solution.py:198
  1359.8 44.0 %reduce-scatter.45.cloned.1.call-done = bf16[256,1024]{1,0:T(8,128)(2,1)} async-done(((bf16[1024,1024]{1,0:T(8,128)(2,1)}), bf16[256,1024]{1,0:T(8,128)(2,1)}) %reduce-scatter.45.cloned.1.call-update) | async-done | bytes 524304 | tf_op jit(solution)/shard_map/reduce_scatter | solution.py:183
  1410.0 30.6 %reduce-scatter.55.cloned.1.call-done = bf16[128,6]{1,0:T(8,128)(2,1)} async-done(((bf16[1024,6]{1,0:T(8,128)(2,1)}), bf16[128,6]{1,0:T(8,128)(2,1)}) %reduce-scatter.55.cloned.1.call-update) | async-done | bytes 1552
  1441.4 11.8 all-reduce.1
  (407 shorter events, 258.1 us)
Async XLA Ops:
  7.2 55.8 %all-gather.51.cloned.1.call-start = ((), (), s32[]{:S(2)}) async-start(), calls=%async_computation.38 | async-start | bytes 1769472 | tf_op jit(solution)/shard_map/all_gather | solution.py:124
  9.0 77.6 %all-gather.35.cloned.1.call-start = ((), (), s32[]{:S(2)}) async-start(), calls=%async_computation.18 | async-start | bytes 2621440 | tf_op jit(solution)/shard_map/all_gather | solution.py:138
  38.8 113.4 %reduce-scatter.31.cloned.1.call-start = ((), (), s32[]{:S(2)}) async-start(), calls=%async_computation.19 | async-start | bytes 2621440 | tf_op jit(solution)/shard_map/reduce_scatter | solution.py:147
  59.8 47.0 %copy-start.19 = (bf16[1,256,1024]{2,1,0:T(8,128)(2,1)}, bf16[1,256,1024]{2,1,0:T(8,128)(2,1)S(1)}, u32[]{:S(2)}) copy-start(bf16[1,256,1024]{2,1,0:T(8,128)(2,1)S(1)} %all-gather.3) | copy-start | bytes 1572868
  109.6 47.5 %copy-start.30 = (bf16[2,1024,128]{2,1,0:T(8,128)(2,1)S(1)}, bf16[2,1024,128]{2,1,0:T(8,128)(2,1)}, u32[]{:S(2)}) copy-start(bf16[2,1024,128]{2,1,0:T(8,128)(2,1)} %param.25) | copy-start | bytes 1572868
  109.6 48.4 %copy-start.50 = (bf16[2,1024]{1,0:T(2,128)(2,1)S(1)}, bf16[2,1024]{1,0:T(2,128)(2,1)}, u32[]{:S(2)}) copy-start(bf16[2,1024]{1,0:T(2,128)(2,1)} %param.24) | copy-start | bytes 12292
  109.7 71.3 %all-gather.53.cloned.1.call-start = ((), (), s32[]{:S(2)}) async-start(), calls=%async_computation.39 | async-start | bytes 2359296 | tf_op jit(solution)/shard_map/all_gather | solution.py:128
  110.5 118.1 %all-gather.37.cloned.1.call-start = ((), (), s32[]{:S(2)}) async-start(), calls=%async_computation.20 | async-start | bytes 2621440 | tf_op jit(solution)/shard_map/all_gather | solution.py:138
  133.3 101.9 %copy-start.36 = (f32[1,1024]{1,0:T(1,128)}, f32[1,1024]{1,0:T(1,128)S(1)}, u32[]{:S(2)}) copy-start(f32[1,1024]{1,0:T(1,128)S(1)} %convert_element_type.449) | copy-start | bytes 12292
  153.5 81.6 %copy-start.48 = (f32[256]{0:T(256)}, f32[256]{0:T(256)S(1)}, u32[]{:S(2)}) copy-start(f32[256]{0:T(256)S(1)} %broadcast_multiply_fusion.10) | copy-start | bytes 3076
  154.9 80.2 %copy-start.53 = (f32[256]{0:T(256)}, f32[256]{0:T(256)S(1)}, u32[]{:S(2)}) copy-start(f32[256]{0:T(256)S(1)} %add_rsqrt_fusion.2) | copy-start | bytes 3076
  157.1 100.8 %all-gather.55.cloned.1.call-start = ((), (), s32[]{:S(2)}) async-start(), calls=%async_computation.40 | async-start | bytes 2359296 | tf_op jit(solution)/shard_map/all_gather | solution.py:129
  158.0 150.7 %reduce-scatter.33.cloned.1.call-start = ((), (), s32[]{:S(2)}) async-start(), calls=%async_computation.21 | async-start | bytes 2621440 | tf_op jit(solution)/shard_map/reduce_scatter | solution.py:147
  257.9 50.8 %copy-start.5 = (bf16[256,1024]{1,0:T(8,128)(2,1)S(1)}, bf16[256,1024]{1,0:T(8,128)(2,1)}, u32[]{:S(2)}) copy-start(bf16[256,1024]{1,0:T(8,128)(2,1)} %reduce-scatter.31.cloned.1.call-done) | copy-start | bytes 1572868
  265.0 70.9 %all-gather.57.cloned.1.call-start = ((), (), s32[]{:S(2)}) async-start(), calls=%async_computation.41 | async-start | bytes 1769472 | tf_op jit(solution)/shard_map/all_gather | solution.py:124
  265.7 117.9 %all-gather.39.cloned.1.call-start = ((), (), s32[]{:S(2)}) async-start(), calls=%async_computation.22 | async-start | bytes 2621440 | tf_op jit(solution)/shard_map/all_gather | solution.py:138
  311.5 136.0 %reduce-scatter.35.cloned.1.call-start = ((), (), s32[]{:S(2)}) async-start(), calls=%async_computation.23 | async-start | bytes 2621440 | tf_op jit(solution)/shard_map/reduce_scatter | solution.py:147
  329.4 73.3 %copy-start.25 = (bf16[1,256,1024]{2,1,0:T(8,128)(2,1)}, bf16[1,256,1024]{2,1,0:T(8,128)(2,1)S(1)}, u32[]{:S(2)}) copy-start(bf16[1,256,1024]{2,1,0:T(8,128)(2,1)S(1)} %all-gather.13) | copy-start | bytes 1572868
  404.8 72.1 %all-gather.59.cloned.1.call-start = ((), (), s32[]{:S(2)}) async-start(), calls=%async_computation.42 | async-start | bytes 2359296 | tf_op jit(solution)/shard_map/all_gather | solution.py:128
  405.6 119.0 %all-gather.41.cloned.1.call-start = ((), (), s32[]{:S(2)}) async-start(), calls=%async_computation.24 | async-start | bytes 2621440 | tf_op jit(solution)/shard_map/all_gather | solution.py:138
  450.0 120.6 %all-gather.43.cloned.1.call-start = ((), (), s32[]{:S(2)}) async-start(), calls=%async_computation.26 | async-start | bytes 2621440 | tf_op jit(solution)/shard_map/all_gather | solution.py:160
  450.8 149.1 %all-gather.61.cloned.1.call-start = ((), (), s32[]{:S(2)}) async-start(), calls=%async_computation.43 | async-start | bytes 2359296 | tf_op jit(solution)/shard_map/all_gather | solution.py:129
  451.4 206.1 %reduce-scatter.39.cloned.1.call-start = ((), (), s32[]{:S(2)}) async-start(), calls=%async_computation.27 | async-start | bytes 2621440 | tf_op jit(solution)/shard_map/reduce_scatter | solution.py:183
  613.7 88.8 %reduce-scatter.37.cloned.1.call-start = ((), (), s32[]{:S(2)}) async-start(), calls=%async_computation.25 | async-start | bytes 2621440 | tf_op jit(solution)/shard_map/reduce_scatter | solution.py:147
  620.7 132.5 %all-gather.45.cloned.1.call-start = ((), (), s32[]{:S(2)}) async-start(), calls=%async_computation.28 | async-start | bytes 2621440 | tf_op jit(solution)/shard_map/all_gather | solution.py:160
  708.3 122.5 %reduce-scatter.41.cloned.1.call-start = ((), (), s32[]{:S(2)}) async-start(), calls=%async_computation.29 | async-start | bytes 2621440 | tf_op jit(solution)/shard_map/reduce_scatter | solution.py:183
  788.2 92.0 %all-gather.47.cloned.1.call-start = ((), (), s32[]{:S(2)}) async-start(), calls=%async_computation.30 | async-start | bytes 2621440 | tf_op jit(solution)/shard_map/all_gather | solution.py:160
  835.2 54.4 %copy-start.62 = (bf16[1,1024,1024]{2,1,0:T(8,128)(2,1)S(1)}, bf16[1,1024,1024]{2,1,0:T(8,128)(2,1)}, u32[]{:S(2)}) copy-start(bf16[1,1024,1024]{2,1,0:T(8,128)(2,1)} %all-gather.53.cloned.1.call-done) | copy-start | bytes 6291460
  835.2 100.6 %reduce-scatter.43.cloned.1.call-start = ((), (), s32[]{:S(2)}) async-start(), calls=%async_computation.31 | async-start | bytes 2621440 | tf_op jit(solution)/shard_map/reduce_scatter | solution.py:183
  889.5 46.3 %copy-start.49 = (f32[256]{0:T(256)S(1)}, f32[256]{0:T(256)}, u32[]{:S(2)}) copy-start(f32[256]{0:T(256)} %copy-done.48) | copy-start | bytes 3076
  889.5 46.3 %copy-start.54 = (f32[256]{0:T(256)S(1)}, f32[256]{0:T(256)}, u32[]{:S(2)}) copy-start(f32[256]{0:T(256)} %copy-done.53) | copy-start | bytes 3076
  893.3 92.2 %all-gather.49.cloned.1.call-start = ((), (), s32[]{:S(2)}) async-start(), calls=%async_computation.32 | async-start | bytes 2621440 | tf_op jit(solution)/shard_map/all_gather | solution.py:160
  940.5 92.0 %reduce-scatter.65.cloned.1.call-start = ((), (), s32[]{:S(2)}) async-start(), calls=%async_computation.49 | async-start | bytes 2359296
  949.3 117.4 %reduce-scatter.61.cloned.1.call-start = ((), (), s32[]{:S(2)}) async-start(), calls=%async_computation.47 | async-start | bytes 589824
  952.6 151.2 %reduce-scatter.57.cloned.1.call-start = ((), (), s32[]{:S(2)}) async-start(), calls=%async_computation.45 | async-start | bytes 294912
  953.7 194.5 %reduce-scatter.63.cloned.1.call-start = ((), (), s32[]{:S(2)}) async-start(), calls=%async_computation.48 | async-start | bytes 2359296
  962.3 230.2 %reduce-scatter.53.cloned.1.call-start = ((), (), s32[]{:S(2)}) async-start(), calls=%async_computation.37 | async-start | bytes 2359296 | tf_op jit(solution)/shard_map/reduce_scatter | solution.py:204
  968.5 268.3 %reduce-scatter.51.cloned.1.call-start = ((), (), s32[]{:S(2)}) async-start(), calls=%async_computation.36 | async-start | bytes 2359296 | tf_op jit(solution)/shard_map/reduce_scatter | solution.py:204
  973.9 300.7 %reduce-scatter.59.cloned.1.call-start = ((), (), s32[]{:S(2)}) async-start(), calls=%async_computation.46 | async-start | bytes 589824
  988.8 327.5 %reduce-scatter.49.cloned.1.call-start = ((), (), s32[]{:S(2)}) async-start(), calls=%async_computation.35 | async-start | bytes 1769472 | tf_op jit(solution)/shard_map/reduce_scatter | solution.py:198
  993.7 364.2 %reduce-scatter.47.cloned.1.call-start = ((), (), s32[]{:S(2)}) async-start(), calls=%async_computation.34 | async-start | bytes 1769472 | tf_op jit(solution)/shard_map/reduce_scatter | solution.py:198
  1027.4 376.4 %reduce-scatter.45.cloned.1.call-start = ((), (), s32[]{:S(2)}) async-start(), calls=%async_computation.33 | async-start | bytes 2621440 | tf_op jit(solution)/shard_map/reduce_scatter | solution.py:183
  1032.3 207.7 %copy-start.55 = (f32[1024]{0:T(1024)S(1)}, f32[1024]{0:T(1024)}, u32[]{:S(2)}) copy-start(f32[1024]{0:T(1024)} %get-tuple-element.180) | copy-start | bytes 12292
  1032.3 372.6 %copy-start.35 = (f32[1,1024]{1,0:T(1,128)S(1)}, f32[1,1024]{1,0:T(1,128)}, u32[]{:S(2)}) copy-start(f32[1,1024]{1,0:T(1,128)} %copy-done.34) | copy-start | bytes 12292
  1032.3 372.7 %copy-start.47 = (f32[256]{0:T(256)S(1)}, f32[256]{0:T(256)}, u32[]{:S(2)}) copy-start(f32[256]{0:T(256)} %copy-done.46) | copy-start | bytes 3076
  1032.3 372.7 %copy-start.52 = (f32[256]{0:T(256)S(1)}, f32[256]{0:T(256)}, u32[]{:S(2)}) copy-start(f32[256]{0:T(256)} %copy-done.51) | copy-start | bytes 3076
  1032.4 408.2 %reduce-scatter.55.cloned.1.call-start = ((), (), s32[]{:S(2)}) async-start(), calls=%async_computation.44 | async-start | bytes 294912
  1032.4 375.1 %copy-start.10 = (f32[256,1024]{1,0:T(8,128)S(1)}, f32[256,1024]{1,0:T(8,128)}, u32[]{:S(2)}) copy-start(f32[256,1024]{1,0:T(8,128)} %get-tuple-element.112) | copy-start | bytes 3145732
  (59 other events, 655.3 us)
Sparse Core Ops, SparseCore 0:
  10.4 28.2 all-gather.50
  40.9 45.6 all-gather.34
  109.8 42.4 reduce-scatter.30
  154.0 26.9 all-gather.52
  183.0 45.6 all-gather.36
  231.0 26.8 all-gather.54
  265.1 43.5 reduce-scatter.32
  310.6 25.1 all-gather.56
  338.0 45.6 all-gather.38
  405.0 42.4 reduce-scatter.34
  449.9 26.9 all-gather.58
  478.9 45.6 all-gather.40
  526.2 44.4 all-gather.42
  573.0 26.8 all-gather.60
  613.8 43.6 reduce-scatter.38
  659.6 42.8 reduce-scatter.36
  708.4 44.8 all-gather.44
  788.3 42.4 reduce-scatter.40
  835.3 44.8 all-gather.46
  893.4 42.4 reduce-scatter.42
  940.6 44.8 all-gather.48
  988.8 39.9 reduce-scatter.64
  1032.4 34.2 reduce-scatter.60
  1070.1 33.6 reduce-scatter.56
  1107.1 41.0 reduce-scatter.62
  1151.3 41.1 reduce-scatter.52
  1195.6 41.0 reduce-scatter.50
  1240.4 34.1 reduce-scatter.58
  1277.9 38.3 reduce-scatter.48
  1319.5 38.3 reduce-scatter.46
  1360.2 43.6 reduce-scatter.44
  1407.7 32.8 reduce-scatter.54
where the time goes:
time: 1470 us; the launch traced here: 1460 us
  waiting for transfers between devices  964 us (66%)
  blocking collectives  208 us (14%)
  matrix products  171 us (12%)
  other arithmetic  66.3 us (5%)
  local copies, waits for them, and re-layouts  32.9 us (2%)
  between operations  16.1 us (1%)
    all_gather x4, waiting for transfers between devices, spread_rows(): lax.all_gather(normed, 'col', axis=0, tiled=True)  167 us
    unnamed x38, waiting for transfers between devices  156 us
    reduce_scatter x4, waiting for transfers between devices, input_rows(): lax.psum_scatter(jnp.einsum('nf,df->nd', lax.dynamic_slice_in_dim(upstrea...  155 us
    all_gather x4, waiting for transfers between devices, pull_rows(): shard_rows = lax.all_gather(upstream, 'col', axis=0, tiled=True)  141 us
    reduce_scatter x2, waiting for transfers between devices, reduce_grads(): lax.psum_scatter(up_grad.astype(jnp.bfloat16), ('dp', 'row'), scatter_dim...  87.4 us
    reduce_scatter x2, waiting for transfers between devices, reduce_grads(): lax.psum_scatter(qkv_grad.astype(jnp.bfloat16), ('dp', 'row'), scatter_di...  81.5 us
    reduce_scatter x4, waiting for transfers between devices, branch_rows(): lax.psum_scatter(jnp.dot(lax.dynamic_slice_in_dim(left, jnp.int32(0), lax...  70.1 us
    all_gather x2, waiting for transfers between devices, gather_weights(): lax.all_gather(down_w[layer_index], ('dp', 'row'), axis=1, tiled=True)  52 us
  transfers between devices with their start and end apart: 32, of which 30 were waited for; matrix products, arithmetic and copies ran while one was open for 9% of the time, Pallas kernels for 0%

commit v1 on v0

v1 whole, which is shorter than its diff:
```python
import functools

import jax
import jax.numpy as jnp
from jax import lax
from jax.experimental import pallas as pl
from jax.experimental.pallas import tpu as pltpu
from jax.sharding import Mesh
from jax.sharding import PartitionSpec as P

HEADS = 16
HEAD_DIM = 64
LAYERS = 2

epsilon = 1e-05
gelu_scale = 0.7978845608028654
gelu_cube = 0.044715
F32 = jnp.float32
BF16 = jnp.bfloat16
SWAP = [(0, 1), (1, 0)]


def attend_kernel(heads, blk, nblk, ids_ref, slope_ref, p_ref, o_ref, lse_ref, k_sc, v_sc):
    q_id = ids_ref[0]
    width = heads * HEAD_DIM
    for j in range(nblk):
        src = pl.ds(pl.multiple_of((j ^ q_id) * blk, blk), blk)
        k_sc[j * blk:(j + 1) * blk, :] = p_ref[src, width:2 * width]
        v_sc[j * blk:(j + 1) * blk, :] = p_ref[src, 2 * width:]
    lanes = lax.broadcasted_iota(jnp.int32, (blk, width), 1) // HEAD_DIM
    row = lax.broadcasted_iota(jnp.int32, (blk, blk), 0)
    col = lax.broadcasted_iota(jnp.int32, (blk, blk), 1)
    lse_lane = lax.broadcasted_iota(jnp.int32, (blk, 128), 1)
    for i in range(nblk):
        dst = pl.ds(pl.multiple_of((i ^ q_id) * blk, blk), blk)
        klen = (i + 1) * blk
        kpos = lax.broadcasted_iota(jnp.int32, (1, klen), 1).astype(F32)
        q = p_ref[dst, 0:width] * BF16(HEAD_DIM ** -0.5)

        def head(h, carry):
            out, lse = carry
            qm = jnp.where(lanes == h, q, BF16(0))
            s = lax.dot_general(qm, k_sc[0:klen, :], (((1,), (1,)), ((), ())),
                                preferred_element_type=F32)
            s = s + kpos * slope_ref[h]
            last = jnp.where(col <= row, s[:, klen - blk:], -1e30)
            s = last if i == 0 else jnp.concatenate([s[:, :klen - blk], last], axis=1)
            peak = jnp.max(s, axis=-1, keepdims=True)
            e = jnp.exp(s - peak)
            total = jnp.sum(e, axis=-1, keepdims=True)
            mixed = jnp.dot(e.astype(BF16), v_sc[0:klen, :], preferred_element_type=F32)
            mixed = mixed * (1.0 / total)
            return (jnp.where(lanes == h, mixed, out),
                    jnp.where(lse_lane == h, peak + jnp.log(total), lse))

        out, lse = lax.fori_loop(0, heads, head, (jnp.zeros((blk, width), F32), jnp.zeros((blk, 128), F32)))
        o_ref[dst, :] = out.astype(BF16)
        lse_ref[:, i * blk:(i + 1) * blk] = lse.T[0:8, :]


def attend(packed, ids, slopes, nblk):
    rows, width3 = packed.shape
    width = width3 // 3
    heads = width // HEAD_DIM
    blk = rows // nblk
    return pl.pallas_call(
        functools.partial(attend_kernel, heads, blk, nblk),
        out_shape=(jax.ShapeDtypeStruct((rows, width), BF16), jax.ShapeDtypeStruct((8, rows), F32)),
        in_specs=[pl.BlockSpec(memory_space=pltpu.SMEM), pl.BlockSpec(memory_space=pltpu.SMEM), pl.BlockSpec(memory_space=pltpu.VMEM)],
        out_specs=(pl.BlockSpec(memory_space=pltpu.VMEM), pl.BlockSpec(memory_space=pltpu.VMEM)),
        scratch_shapes=[pltpu.VMEM((rows, width), BF16)] * 2,
        cost_estimate=pl.CostEstimate(flops=12_000_000_000, transcendentals=heads * rows * rows // 2, bytes_accessed=rows * width * 8),
        name="attend",
    )(ids, slopes, packed)


def attend_back_kernel(heads, blk, nblk, ids_ref, slope_ref, p_ref, o_ref, lse_ref, g_ref, out_ref, q_sc, k_sc, v_sc, g_sc, d_sc, dq_sc, dk_sc, dv_sc):
    q_id = ids_ref[0]
    width = heads * HEAD_DIM
    rows = nblk * blk
    pick = (lax.broadcasted_iota(jnp.int32, (8, width), 1) // HEAD_DIM == lax.broadcasted_iota(jnp.int32, (8, width), 0))
    pick = jnp.where(pick, 1.0, 0.0).astype(BF16)
    nt = (((1,), (1,)), ((), ()))
    tn = (((0,), (0,)), ((), ()))
    for j in range(nblk):
        src = pl.ds(pl.multiple_of((j ^ q_id) * blk, blk), blk)
        here = slice(j * blk, (j + 1) * blk)
        q_sc[here, :] = p_ref[src, 0:width] * BF16(HEAD_DIM ** -0.5)
        k_sc[here, :] = p_ref[src, width:2 * width]
        v_sc[here, :] = p_ref[src, 2 * width:]
        g = g_ref[src, :]
        g_sc[here, :] = g
        prod = g.astype(F32) * o_ref[src, :].astype(F32)
        high = prod.astype(BF16)
        rest = (prod - high.astype(F32)).astype(BF16)
        d_sc[:, here] = (lax.dot_general(pick, high, nt, preferred_element_type=F32)
                         + lax.dot_general(pick, rest, nt, preferred_element_type=F32))
    dq_sc[...] = jnp.zeros_like(dq_sc)
    dk_sc[...] = jnp.zeros_like(dk_sc)
    dv_sc[...] = jnp.zeros_like(dv_sc)
    krow = lax.broadcasted_iota(jnp.int32, (blk, blk), 0)
    qcol = lax.broadcasted_iota(jnp.int32, (blk, blk), 1)
    row8 = lax.broadcasted_iota(jnp.int32, (8, rows), 0)

    def head(h, carry):
        slope = slope_ref[h]
        lse_row = jnp.sum(jnp.where(row8 == h, lse_ref[...], 0.0), axis=0, keepdims=True)
        d_row = jnp.sum(jnp.where(row8 == h, d_sc[...], 0.0), axis=0, keepdims=True)
        for j in range(nblk):
            first = j * blk
            n = rows - first
            lane_q = lax.broadcasted_iota(jnp.int32, (n, width), 1) // HEAD_DIM == h
            lane_k = lax.broadcasted_iota(jnp.int32, (blk, width), 1) // HEAD_DIM == h
            qm = jnp.where(lane_q, q_sc[first:, :], BF16(0))
            gm = jnp.where(lane_q, g_sc[first:, :], BF16(0))
            k = k_sc[first:first + blk, :]
            km = jnp.where(lane_k, k, BF16(0))
            s = lax.dot_general(k, qm, nt, preferred_element_type=F32)
            kpos = (lax.broadcasted_iota(jnp.int32, (blk, 1), 0) + first).astype(F32)
            s = (s + kpos * slope) - lse_row[:, first:]
            lead = jnp.where(krow <= qcol, s[:, :blk], -1e30)
            s = lead if n == blk else jnp.concatenate([lead, s[:, blk:]], axis=1)
            p = jnp.exp(s)
            dp = lax.dot_general(v_sc[first:first + blk, :], gm, nt, preferred_element_type=F32)
            ds = (p * (dp - d_row[:, first:])).astype(BF16)
            dv_sc[first:first + blk, :] += jnp.dot(p.astype(BF16), gm, preferred_element_type=F32)
            dk_sc[first:first + blk, :] += jnp.dot(ds, qm, preferred_element_type=F32)
            dq_sc[first:, :] += lax.dot_general(ds, km, tn, preferred_element_type=F32)
        return carry

    lax.fori_loop(0, heads, head, 0)
    for j in range(nblk):
        dst = pl.ds(pl.multiple_of((j ^ q_id) * blk, blk), blk)
        here = slice(j * blk, (j + 1) * blk)
        out_ref[dst, 0:width] = (dq_sc[here, :] * HEAD_DIM ** -0.5).astype(BF16)
        out_ref[dst, width:2 * width] = dk_sc[here, :].astype(BF16)
        out_ref[dst, 2 * width:] = dv_sc[here, :].astype(BF16)


def attend_back(packed, mixed, lse, grad, ids, slopes, nblk):
    rows, width3 = packed.shape
    width = width3 // 3
    heads = width // HEAD_DIM
    blk = rows // nblk
    vm = pl.BlockSpec(memory_space=pltpu.VMEM)
    sm = pl.BlockSpec(memory_space=pltpu.SMEM)
    return pl.pallas_call(
        functools.partial(attend_back_kernel, heads, blk, nblk),
        out_shape=jax.ShapeDtypeStruct((rows, width3), BF16),
        in_specs=[sm, sm, vm, vm, vm, vm],
        out_specs=vm,
        scratch_shapes=[pltpu.VMEM((rows, width), BF16)] * 4 + [pltpu.VMEM((8, rows), F32)] + [pltpu.VMEM((rows, width), F32)] * 3,
        cost_estimate=pl.CostEstimate(flops=24_000_000_000, transcendentals=heads * rows * rows // 2, bytes_accessed=rows * width * 16),
        name="attend_back",
    )(ids, slopes, packed, mixed, lse, grad)


class Paired:
    axes = ("y", "c", "x", "z")
    spec = {"tokens": ("y", "c", "x", "z"), "width": ("y", "c", "x"), "heads": "z"}

    def __init__(self, mesh):
        self.mesh = Mesh(mesh.devices.reshape(-1, 2, mesh.shape["row"], mesh.shape["col"]), self.axes)
        self.places = mesh.shape["col"]

    def move(self, value):
        n = self.places
        pairs = [(a * n + b, b * n + a) for a in range(n) for b in range(n)]
        return lax.ppermute(value, ("c", "x", "z"), pairs)

    def shard(self):
        return lax.axis_index("c") * 2 + lax.axis_index("x")

    def first_block(self):
        return self.shard()

    def enter_width(self, value):
        half = value.shape[-1] // 2
        turned = jnp.concatenate([value[..., half:], value[..., :half]], axis=-1)
        return jnp.where(lax.axis_index("y") == 0, value, turned)

    leave_width = enter_width

    def gather_rows(self, value):
        pair = jnp.concatenate([value, lax.ppermute(value, "x", SWAP)], axis=0)
        return jnp.concatenate([pair, lax.ppermute(pair, "c", SWAP)], axis=0)

    def scatter_rows(self, value):
        half = value.shape[0] // 2
        other = lax.ppermute(value[half:].astype(BF16), "c", SWAP)
        pair = value[:half].astype(F32) + other.astype(F32)
        quarter = half // 2
        other = lax.ppermute(pair[quarter:].astype(BF16), "x", SWAP)
        return pair[:quarter] + other.astype(F32)

    def gather_weight(self, value):
        own = lax.all_gather(value, "z", axis=0, tiled=True)
        return jnp.concatenate([own, lax.ppermute(own, "y", SWAP)], axis=0)

    def scatter_grad(self, value):
        half = value.shape[0] // 2
        other = lax.ppermute(value[half:].astype(BF16), "y", SWAP)
        own = (value[:half] + other.astype(F32)).astype(BF16)
        return lax.psum_scatter(own, "z", scatter_dimension=0, tiled=True)

    def share_slot(self):
        return lax.axis_index("z")

    def width_slot(self):
        return lax.axis_index("y") * 4 + lax.axis_index("c") * 2 + lax.axis_index("x")


class Plain:
    spec = {"tokens": ("dp", "row", "col"), "width": ("dp", "row"), "heads": "col"}
    axes = ("dp", "row", "col")

    def __init__(self, mesh):
        self.mesh = mesh
        self.places = mesh.shape["col"]

    def move(self, value):
        return value

    def shard(self):
        return lax.axis_index("col")

    def first_block(self):
        return jnp.int32(0)

    def enter_width(self, value):
        return value

    leave_width = enter_width

    def gather_rows(self, value):
        return lax.all_gather(value, "col", axis=0, tiled=True)

    def scatter_rows(self, value):
        return lax.psum_scatter(value.astype(BF16), "col", scatter_dimension=0, tiled=True).astype(F32)

    def gather_weight(self, value):
        return lax.all_gather(value, ("dp", "row"), axis=0, tiled=True)

    def scatter_grad(self, value):
        return lax.psum_scatter(value.astype(BF16), ("dp", "row"), scatter_dimension=0, tiled=True)

    def share_slot(self):
        return lax.axis_index("col")

    def width_slot(self):
        return lax.axis_index(("dp", "row"))


def normalize(values):
    center = jnp.mean(values, axis=-1, keepdims=True)
    centered = values - center
    spread = jnp.mean(centered * centered, axis=-1, keepdims=True)
    inverse = lax.rsqrt(spread + epsilon)
    return (centered * inverse, inverse)


def norm_backward(upstream, normal, inverse, gain_vec):
    scaled = upstream * gain_vec
    mean_first = jnp.mean(scaled, axis=-1, keepdims=True)
    second = jnp.mean(scaled * normal, axis=-1, keepdims=True)
    return inverse * (scaled - mean_first - normal * second)


def gelu_parts(pre_act):
    tangent = jnp.tanh(gelu_scale * (pre_act + gelu_cube * pre_act * pre_act * pre_act))
    result = 0.5 * pre_act * (1.0 + tangent)
    derivative = 0.5 * (1.0 + tangent) + 0.5 * pre_act * (1.0 - tangent * tangent) * gelu_scale * (
        1.0 + 3.0 * gelu_cube * pre_act * pre_act
    )
    return (result, derivative)


def dot_nn(left, right):
    return jnp.dot(left, right, preferred_element_type=F32)


def dot_nt(left, right):
    return lax.dot_general(left, right, (((1,), (1,)), ((), ())), preferred_element_type=F32)


def dot_tn(left, right):
    return lax.dot_general(left, right, (((0,), (0,)), ((), ())), preferred_element_type=F32)


def by_kind(weight):
    rows, columns = weight.shape
    return weight.reshape(rows, -1, 3, HEAD_DIM).swapaxes(1, 2).reshape(rows, columns)


def by_head(weight):
    rows, columns = weight.shape
    return weight.reshape(rows, 3, -1, HEAD_DIM).swapaxes(1, 2).reshape(rows, columns)


def local(
    plan,
    x_in,
    ln1_gain,
    ln1_bias,
    w_qkv,
    b_qv,
    w_out,
    b_out,
    ln2_gain,
    ln2_bias,
    w_up,
    b_up,
    w_down,
    b_down,
    cotangent,
):
    places = plan.places
    local_heads = HEADS // places
    width = local_heads * HEAD_DIM
    shard = plan.shard()
    ids = plan.first_block().reshape(1).astype(jnp.int32)
    head_order = (shard * local_heads + jnp.arange(local_heads, dtype=jnp.int32)).astype(F32)
    slopes = jnp.exp2(-8.0 * (head_order + 1.0) / HEADS)

    stream = plan.enter_width(plan.move(x_in)).astype(F32)
    vectors = jnp.concatenate([ln1_gain, ln1_bias, b_out, ln2_gain, ln2_bias, b_down], axis=0)
    head_parts = jnp.concatenate([b_qv, b_up], axis=1)
    small = jnp.concatenate([vectors.reshape(-1), head_parts.reshape(-1)]).reshape(-1, 128)
    small = plan.move(small).reshape(-1)
    vectors = plan.gather_weight(small[: vectors.size].reshape(vectors.shape).T).T.astype(F32)
    head_parts = small[vectors.shape[0] * ln1_gain.shape[1] :].reshape(head_parts.shape).astype(F32)

    blocks = []
    for layer in range(LAYERS):
        attn_w = plan.move(jnp.concatenate([by_kind(w_qkv[layer]), w_out[layer].T], axis=1))
        blocks.append((attn_w, plan.move(w_up[layer]), plan.move(w_down[layer].T)))
    upstream_in = plan.move(cotangent)

    saved = []
    for layer in range(LAYERS):
        gain_one, bias_one, out_bias, gain_two, bias_two, down_bias = [
            vectors[LAYERS * kind + layer][None] for kind in range(6)
        ]
        attn_w, up_w, down_w = [plan.gather_weight(block) for block in blocks[layer]]
        qkv_w, out_w = attn_w[:, : 3 * width], attn_w[:, 3 * width :]
        pair = head_parts[layer, : 2 * width].reshape(local_heads, 2, HEAD_DIM)
        merged = jnp.concatenate(
            [pair[:, 0].reshape(-1), jnp.zeros((width,), F32), pair[:, 1].reshape(-1)]
        )
        up_bias = head_parts[layer, 2 * width :]
        normal_one, inverse_one = normalize(stream)
        rows_one = plan.gather_rows((normal_one * gain_one + bias_one).astype(BF16))
        packed = (dot_nn(rows_one, qkv_w) + merged).astype(BF16)
        mixed, log_totals = attend(packed, ids, slopes, places)
        middle = stream + (plan.scatter_rows(dot_nt(mixed, out_w).astype(BF16)) + out_bias)
        normal_two, inverse_two = normalize(middle)
        rows_two = plan.gather_rows((normal_two * gain_two + bias_two).astype(BF16))
        result, derivative = gelu_parts(dot_nn(rows_two, up_w) + up_bias)
        activated = result.astype(BF16)
        derivative = derivative.astype(BF16)
        stream = middle + (plan.scatter_rows(dot_nt(activated, down_w).astype(BF16)) + down_bias)
        saved.append(
            (
                normal_one,
                inverse_one,
                rows_one,
                packed,
                mixed,
                log_totals,
                normal_two,
                inverse_two,
                rows_two,
                activated,
                derivative,
                qkv_w,
                out_w,
                up_w,
                down_w,
                gain_one,
                gain_two,
            )
        )
    out_stream = plan.move(plan.leave_width(stream.astype(BF16)))

    upstream = plan.enter_width(upstream_in).astype(F32)
    shares = [None] * LAYERS
    vector_sums = [None] * LAYERS
    head_sums = [None] * LAYERS
    for layer in reversed(range(LAYERS)):
        (
            normal_one,
            inverse_one,
            rows_one,
            packed,
            mixed,
            log_totals,
            normal_two,
            inverse_two,
            rows_two,
            activated,
            derivative,
            qkv_w,
            out_w,
            up_w,
            down_w,
            gain_one,
            gain_two,
        ) = saved[layer]
        branch_grad = upstream.astype(BF16)
        down_bias_grad = jnp.sum(branch_grad.astype(F32), axis=0)
        branch_rows = plan.gather_rows(branch_grad)
        pre_grad = (dot_nn(branch_rows, down_w) * derivative.astype(F32)).astype(BF16)
        normed_grad = plan.scatter_rows(dot_nt(pre_grad, up_w).astype(BF16))
        down_grad = plan.scatter_grad(dot_tn(branch_rows, activated).astype(BF16))
        up_grad = plan.scatter_grad(dot_tn(rows_two, pre_grad).astype(BF16))
        up_bias_grad = jnp.sum(pre_grad.astype(F32), axis=0)
        gain_two_grad = jnp.sum(normed_grad * normal_two, axis=0)
        bias_two_grad = jnp.sum(normed_grad, axis=0)
        middle_grad = upstream + norm_backward(normed_grad, normal_two, inverse_two, gain_two)
        attn_grad = middle_grad.astype(BF16)
        out_bias_grad = jnp.sum(attn_grad.astype(F32), axis=0)
        attn_rows = plan.gather_rows(attn_grad)
        mixed_grad = dot_nn(attn_rows, out_w).astype(BF16)
        packed_grad = attend_back(packed, mixed, log_totals, mixed_grad, ids, slopes, places)
        first_grad = plan.scatter_rows(dot_nt(packed_grad, qkv_w).astype(BF16))
        attn_share = plan.scatter_grad(
            jnp.concatenate([dot_tn(rows_one, packed_grad).astype(BF16), dot_tn(attn_rows, mixed).astype(BF16)], axis=1)
        )
        column_sums = jnp.sum(packed_grad.astype(F32), axis=0)
        qv_bias_grad = jnp.concatenate(
            [
                column_sums[:width].reshape(local_heads, 1, HEAD_DIM),
                column_sums[2 * width :].reshape(local_heads, 1, HEAD_DIM),
            ],
            axis=1,
        ).reshape(-1)
        gain_one_grad = jnp.sum(first_grad * normal_one, axis=0)
        bias_one_grad = jnp.sum(first_grad, axis=0)
        upstream = middle_grad + norm_backward(first_grad, normal_one, inverse_one, gain_one)
        vector_sums[layer] = jnp.stack(
            [gain_one_grad, bias_one_grad, out_bias_grad, gain_two_grad, bias_two_grad, down_bias_grad]
        )
        head_sums[layer] = jnp.concatenate([qv_bias_grad, up_bias_grad])
        attn_share = plan.move(attn_share).astype(F32)
        shares[layer] = (
            by_head(attn_share[:, : 3 * width]),
            attn_share[:, 3 * width :].T,
            plan.move(up_grad).astype(F32),
            plan.move(down_grad).astype(F32).T,
        )
    grad_in = plan.move(plan.leave_width(upstream.astype(BF16))).astype(F32)

    vector_rows = plan.leave_width(jnp.stack(vector_sums))
    head_rows = jnp.stack(head_sums)
    slots = jnp.where(
        (jnp.arange(places, dtype=jnp.int32) == shard)[:, None, None], head_rows[None], 0.0
    )
    totals = lax.psum(
        jnp.concatenate([vector_rows.reshape(-1), slots.reshape(-1)]).reshape(-1, 1024), plan.axes
    ).reshape(-1)
    vector_rows = totals[: vector_rows.size].reshape(vector_rows.shape)
    slots = totals[vector_rows.size :].reshape(slots.shape)
    own = ln1_gain.shape[1]
    vector_rows = lax.dynamic_slice_in_dim(vector_rows, plan.width_slot() * own, own, 2)
    head_rows = lax.dynamic_index_in_dim(slots, plan.share_slot(), 0, keepdims=False)

    def stacked(member):
        return jnp.stack([shares[layer][member] for layer in range(LAYERS)])

    return (
        out_stream,
        grad_in,
        vector_rows[:, 0],
        vector_rows[:, 1],
        stacked(0),
        head_rows[:, : 2 * width],
        stacked(1),
        vector_rows[:, 2],
        vector_rows[:, 3],
        vector_rows[:, 4],
        stacked(2),
        head_rows[:, 2 * width :],
        stacked(3),
        vector_rows[:, 5],
    )


def solution(mesh):
    shape = mesh.shape
    paired = shape["dp"] == 4 and shape["row"] == 2 and shape["col"] == 4
    plan = Paired(mesh) if paired else Plain(mesh)
    tokens, wide, heads = plan.spec["tokens"], plan.spec["width"], plan.spec["heads"]
    rows = P(tokens, None)
    vector = P(None, wide)
    inward = P(None, wide, heads)
    outward = P(None, heads, wide)
    per_head = P(None, heads)
    return jax.shard_map(
        functools.partial(local, plan),
        mesh=plan.mesh,
        in_specs=(
            rows, vector, vector, inward, per_head, outward, vector,
            vector, vector, inward, per_head, outward, vector, rows,
        ),
        out_specs=(
            rows, rows, vector, vector, inward, per_head, outward, vector,
            vector, vector, inward, per_head, outward, vector,
        ),
        check_vma=False,
    )
```

time: 1470 us -> 961 us (0.65)
  waiting for transfers between devices: 964 us -> 506 us
  blocking collectives: 208 us -> 28.7 us
  starting transfers between devices: 2.75 us -> 148 us
  matrix products: 171 us -> 80.6 us
  Pallas kernels: 0 us -> 52.5 us
  local copies, waits for them, and re-layouts: 32.9 us -> 52.7 us
    reduce_scatter x12 -> x4, waiting for transfers between devices: 394 us -> 0.03 us  [scatter_grad(): return lax.psum_scatter(own, 'z', scatter_dimension=0, tiled=True)]
    all_gather x14 -> x6, waiting for transfers between devices: 414 us -> 103 us  [gather_weight(): own = lax.all_gather(value, 'z', axis=0, tiled=True)]
    ppermute x0 -> x62, waiting for transfers between devices: none -> 261 us  [the longest x7 84.8 us: gather_weight(): return jnp.concatenate([own, lax.ppermute(own, 'y', SWAP)], axis=0)]
    ppermute x0 -> x62, starting transfers between devices: none -> 146 us  [the longest x8 59.8 us: gather_rows(): pair = jnp.concatenate([value, lax.ppermute(value, 'x', SWAP)], axis=0)]
    all_gather x14 -> x1, blocking collectives: 172 us -> 28.7 us  [gather_weight(): own = lax.all_gather(value, 'z', axis=0, tiled=True)]
    unnamed x38 -> x15, waiting for transfers between devices: 156 us -> 29.8 us
    psum x0 -> x1, waiting for transfers between devices: none -> 111 us  [local(): lax.psum(jnp.concatenate([vector_rows.reshape(-1), slots.reshape(-1)]).re...]
    dot_general x48 -> x24, matrix products: 171 us -> 80.6 us  [the longest x8 34.6 us: dot_nn(): return jnp.dot(left, right, preferred_element_type=F32)]
  transfers between devices with their start and end apart: 32 -> 75, of which waited for: 30 -> 33; matrix products, arithmetic and copies ran while one was open for 9% -> 14% of each run, Pallas kernels for 0% -> 1%
where the time goes in v1:
time: 961 us; the launch traced here: 943 us
  waiting for transfers between devices  506 us (53%)
  starting transfers between devices  148 us (15%)
  matrix products  80.6 us (8%)
  other arithmetic  59 us (6%)
  local copies, waits for them, and re-layouts  52.7 us (5%)
  Pallas kernels  52.5 us (5%)
  blocking collectives  28.7 us (3%)
  between operations  16.3 us (2%)
    psum x1, waiting for transfers between devices, local(): lax.psum(jnp.concatenate([vector_rows.reshape(-1), slots.reshape(-1)]).re...  111 us
    all_gather x6, waiting for transfers between devices, gather_weight(): own = lax.all_gather(value, 'z', axis=0, tiled=True)  103 us
    ppermute x7, waiting for transfers between devices, gather_weight(): return jnp.concatenate([own, lax.ppermute(own, 'y', SWAP)], axis=0)  84.8 us
    ppermute x6, waiting for transfers between devices, scatter_grad(): other = lax.ppermute(value[half:].astype(BF16), 'y', SWAP)  78.3 us
    ppermute x8, waiting for transfers between devices, scatter_rows(): other = lax.ppermute(pair[quarter:].astype(BF16), 'x', SWAP)  64.5 us
    ppermute x8, starting transfers between devices, gather_rows(): pair = jnp.concatenate([value, lax.ppermute(value, 'x', SWAP)], axis=0)  59.8 us
    ppermute x8, starting transfers between devices, scatter_rows(): other = lax.ppermute(pair[quarter:].astype(BF16), 'x', SWAP)  37.7 us
    dot_general x8, matrix products, dot_nn(): return jnp.dot(left, right, preferred_element_type=F32)  34.6 us
  transfers between devices with their start and end apart: 75, of which 33 were waited for; matrix products, arithmetic and copies ran while one was open for 14% of the time, Pallas kernels for 1%

profile of v1, /device:TPU:0, one launch (start us, length us, event | category | flops | bytes accessed | tf_op | source)
XLA Modules:
  0.0 943.4 jit_solution(9595797374435089090)
XLA Ops:
  13.9 28.7 %all_gather.21 = bf16[512,12]{0,1:T(8,128)(2,1)S(1)} all-gather(bf16[128,12]{0,1:T(8,128)(2,1)S(1)} %slice_bitcast_fusion.8), channel_id=1, replica_groups=mesh['y'=2,'c'=2,'x'=2,'z'=4] {'z'}, dimensions={0}, use_global_device_ids=true | all-gather | bytes 15360 | tf_op jit(solution)/shard_map/all_gather | solution.py:197
  48.1 10.3 %collective-permute-start.3 = (bf16[256,1024]{1,0:T(8,128)(2,1)S(1)}, bf16[256,1024]{1,0:T(8,128)(2,1)}, u32[]{:S(2)}, u32[]{:S(2)}) collective-permute-start(bf16[256,1024]{1,0:T(8,128)(2,1)S(1)} %fusion.23), channel_id=1, source_target_pairs={{0,4},{4,0},{1,5},{5,1},{2,6},{6,2},{3,7},{7,3},{8,12},{12,8},{9,1... | collective-permute-start | bytes 1572872 | tf_op jit(solution)/shard_map/ppermute | solution.py:185
  58.4 25.3 %all-gather.7.cloned.1.call-done = bf16[512,1024]{0,1:T(8,128)(2,1)} async-done(((bf16[128,1024]{0,1:T(8,128)(2,1)}), bf16[512,1024]{0,1:T(8,128)(2,1)}) %all-gather.7.cloned.1.call-update) | async-done | bytes 1048592 | tf_op jit(solution)/shard_map/all_gather | solution.py:197
  87.8 20.1 %collective-permute-done.6 = bf16[512,1024]{0,1:T(8,128)(2,1)S(1)} collective-permute-done((bf16[512,1024]{0,1:T(8,128)(2,1)}, bf16[512,1024]{0,1:T(8,128)(2,1)S(1)}, u32[]{:S(2)}, u32[]{:S(2)}) %collective-permute-start.6) | collective-permute-done | bytes 1048608 | tf_op jit(solution)/shard_map/ppermute | solution.py:198
  108.1 5.1 add_convert_fusion.1.p_ref
  113.2 13.9 %attend.2 = (bf16[1024,256]{1,0:T(8,128)(2,1)}, f32[8,1024]{1,0:T(8,128)}) custom-call(s32[1]{0:T(128)} %bitcast.ids_ref, f32[4]{0:T(128)} %multiply_exponential_fusion.slope_ref, bf16[1024,768]{1,0:T(8,128)(2,1)} %add_convert_fusion.1.p_ref), custom_call_target="tpu_custom_call" | custom-call | flops 12000000000 | bytes 2097152 | tf_op jit(solution)/shard_map/attend/pallas_call | solution.py:66
  136.1 15.0 %collective-permute-start.8 = (bf16[256,1024]{1,0:T(8,128)(2,1)S(1)}, bf16[256,1024]{1,0:T(8,128)(2,1)S(1)}, u32[]{:S(2)}, u32[]{:S(2)}) collective-permute-start(bf16[256,1024]{1,0:T(8,128)(2,1)S(1)} %slice.711), channel_id=1, source_target_pairs={{0,4},{4,0},{1,5},{5,1},{2,6},{6,2},{3,7},{7,3},{8,12},{12,8},{9,1... | collective-permute-start | bytes 1572872 | tf_op jit(solution)/shard_map/ppermute | solution.py:193
  153.8 9.0 collective-permute-done.8
  165.4 14.1 %collective-permute-start.9 = (bf16[256,1024]{1,0:T(8,128)(2,1)S(1)}, bf16[256,1024]{1,0:T(8,128)(2,1)S(1)}, u32[]{:S(2)}, u32[]{:S(2)}) collective-permute-start(bf16[256,1024]{1,0:T(8,128)(2,1)S(1)} %add_convert_fusion.10), channel_id=1, source_target_pairs={{0,4},{4,0},{1,5},{5,1},{2,6},{6,2},{3,7},{7,3},{8,12},{12,8},{9,1... | collective-permute-start | bytes 1572872 | tf_op jit(solution)/shard_map/ppermute | solution.py:185
  181.8 29.6 %all-gather.9.cloned.1.call-done = bf16[512,1024]{1,0:T(8,128)(2,1)} async-done(((bf16[128,1024]{1,0:T(8,128)(2,1)}), bf16[512,1024]{1,0:T(8,128)(2,1)}) %all-gather.9.cloned.1.call-update) | async-done | bytes 1048592 | tf_op jit(solution)/shard_map/all_gather | solution.py:197
  214.6 21.4 %collective-permute-done.12 = bf16[512,1024]{1,0:T(8,128)(2,1)S(1)} collective-permute-done((bf16[512,1024]{1,0:T(8,128)(2,1)}, bf16[512,1024]{1,0:T(8,128)(2,1)S(1)}, u32[]{:S(2)}, u32[]{:S(2)}) %collective-permute-start.12) | collective-permute-done | bytes 1048608 | tf_op jit(solution)/shard_map/ppermute | solution.py:198
  249.3 15.2 %collective-permute-done.16 = bf16[256,1024]{1,0:T(8,128)(2,1)S(1)} collective-permute-done((bf16[256,1024]{1,0:T(8,128)(2,1)S(1)}, bf16[256,1024]{1,0:T(8,128)(2,1)S(1)}, u32[]{:S(2)}, u32[]{:S(2)}) %collective-permute-start.16) | collective-permute-done | bytes 524320 | tf_op jit(solution)/shard_map/ppermute | solution.py:193
  269.1 21.6 %all-gather.13.cloned.1.call-done = bf16[512,1024]{0,1:T(8,128)(2,1)} async-done(((bf16[128,1024]{0,1:T(8,128)(2,1)}), bf16[512,1024]{0,1:T(8,128)(2,1)}) %all-gather.13.cloned.1.call-update) | async-done | bytes 1048592 | tf_op jit(solution)/shard_map/all_gather | solution.py:197
  292.1 22.8 %collective-permute-done.20 = bf16[512,1024]{0,1:T(8,128)(2,1)S(1)} collective-permute-done((bf16[512,1024]{0,1:T(8,128)(2,1)}, bf16[512,1024]{0,1:T(8,128)(2,1)S(1)}, u32[]{:S(2)}, u32[]{:S(2)}) %collective-permute-start.20) | collective-permute-done | bytes 1048608 | tf_op jit(solution)/shard_map/ppermute | solution.py:198
  319.4 13.9 %attend.3 = (bf16[1024,256]{1,0:T(8,128)(2,1)}, f32[8,1024]{1,0:T(8,128)}) custom-call(s32[1]{0:T(128)} %bitcast.ids_ref, f32[4]{0:T(128)} %multiply_exponential_fusion.slope_ref, bf16[1024,768]{1,0:T(8,128)(2,1)} %add_convert_fusion.p_ref), custom_call_target="tpu_custom_call" | custom-call | flops 12000000000 | bytes 2097152 | tf_op jit(solution)/shard_map/attend/pallas_call | solution.py:66
  342.4 14.3 %collective-permute-start.22 = (bf16[256,1024]{1,0:T(8,128)(2,1)S(1)}, bf16[256,1024]{1,0:T(8,128)(2,1)S(1)}, u32[]{:S(2)}, u32[]{:S(2)}) collective-permute-start(bf16[256,1024]{1,0:T(8,128)(2,1)S(1)} %slice.709), channel_id=1, source_target_pairs={{0,4},{4,0},{1,5},{5,1},{2,6},{6,2},{3,7},{7,3},{8,12},{12,8},{9,1... | collective-permute-start | bytes 1572872 | tf_op jit(solution)/shard_map/ppermute | solution.py:193
  359.8 8.6 collective-permute-done.22
  371.1 23.2 %collective-permute-start.23 = (bf16[256,1024]{1,0:T(8,128)(2,1)}, bf16[256,1024]{1,0:T(8,128)(2,1)}, u32[]{:S(2)}, u32[]{:S(2)}) collective-permute-start(bf16[256,1024]{1,0:T(8,128)(2,1)} %add_convert_fusion.8), channel_id=1, source_target_pairs={{0,4},{4,0},{1,5},{5,1},{2,6},{6,2},{3,7},{7,3},{8,12},{12,8},{9,1... | collective-permute-start | bytes 1572872 | tf_op jit(solution)/shard_map/ppermute | solution.py:185
  399.7 6.3 collective-permute-start.33
  406.0 23.6 %all-gather.15.cloned.1.call-done = bf16[512,1024]{1,0:T(8,128)(2,1)} async-done(((bf16[128,1024]{1,0:T(8,128)(2,1)}), bf16[512,1024]{1,0:T(8,128)(2,1)}) %all-gather.15.cloned.1.call-update) | async-done | bytes 1048592 | tf_op jit(solution)/shard_map/all_gather | solution.py:197
  435.3 19.0 %collective-permute-done.26 = bf16[512,1024]{1,0:T(8,128)(2,1)S(1)} collective-permute-done((bf16[512,1024]{1,0:T(8,128)(2,1)}, bf16[512,1024]{1,0:T(8,128)(2,1)S(1)}, u32[]{:S(2)}, u32[]{:S(2)}) %collective-permute-start.26) | collective-permute-done | bytes 1048608 | tf_op jit(solution)/shard_map/ppermute | solution.py:198
  454.4 3.9 fusion.41
  458.3 6.9 convert_reduce_fusion
  475.6 11.0 %collective-permute-done.36 = bf16[256,1024]{1,0:T(8,128)(2,1)S(1)} collective-permute-done((bf16[256,1024]{1,0:T(8,128)(2,1)S(1)}, bf16[256,1024]{1,0:T(8,128)(2,1)S(1)}, u32[]{:S(2)}, u32[]{:S(2)}) %collective-permute-start.36) | collective-permute-done | bytes 524320 | tf_op jit(solution)/shard_map/ppermute | solution.py:193
  487.2 9.7 %collective-permute-done.30 = bf16[256,1024]{1,0:T(8,128)(2,1)S(1)} collective-permute-done((bf16[256,1024]{1,0:T(8,128)(2,1)S(1)}, bf16[256,1024]{1,0:T(8,128)(2,1)S(1)}, u32[]{:S(2)}, u32[]{:S(2)}) %collective-permute-start.30) | collective-permute-done | bytes 524320 | tf_op jit(solution)/shard_map/ppermute | solution.py:193
  500.2 11.5 %collective-permute-done.37 = bf16[256,1024]{1,0:T(8,128)(2,1)S(1)} collective-permute-done((bf16[256,1024]{1,0:T(8,128)(2,1)S(1)}, bf16[256,1024]{1,0:T(8,128)(2,1)S(1)}, u32[]{:S(2)}, u32[]{:S(2)}) %collective-permute-start.37) | collective-permute-done | bytes 524320 | tf_op jit(solution)/shard_map/ppermute | solution.py:185
  517.5 12.5 %attend_back.2 = bf16[1024,768]{1,0:T(8,128)(2,1)} custom-call(s32[1]{0:T(128)} %bitcast.ids_ref, f32[4]{0:T(128)} %multiply_exponential_fusion.slope_ref, bf16[1024,768]{1,0:T(8,128)(2,1)} %add_convert_fusion.p_ref, bf16[1024,256]{1,0:T(8,128)(2,1)} %get-tuple-element.19.o_ref, f32[8,1024]{1,0:T(8,128)} %get-tuple-element.20.lse_ref, ...), custom_call_target="tpu_custom_call" | custom-call | flops 24000000000 | bytes 4194304 | tf_op jit(solution)/shard_map/attend_back/pallas_call | solution.py:147
  530.0 3.7 convolution_convert_fusion.11
  542.7 21.0 %collective-permute-done.52 = bf16[512,1024]{0,1:T(8,128)(2,1)S(1)} collective-permute-done((bf16[512,1024]{0,1:T(8,128)(2,1)S(1)}, bf16[512,1024]{0,1:T(8,128)(2,1)S(1)}, u32[]{:S(2)}, u32[]{:S(2)}) %collective-permute-start.52) | collective-permute-done | bytes 1048608 | tf_op jit(solution)/shard_map/ppermute | solution.py:202
  578.1 7.4 collective-permute-done.41
  585.7 15.0 %collective-permute-done.60 = bf16[512,1024]{1,0:T(8,128)(2,1)S(1)} collective-permute-done((bf16[512,1024]{1,0:T(8,128)(2,1)S(1)}, bf16[512,1024]{1,0:T(8,128)(2,1)S(1)}, u32[]{:S(2)}, u32[]{:S(2)}) %collective-permute-start.60) | collective-permute-done | bytes 1048608 | tf_op jit(solution)/shard_map/ppermute | solution.py:202
  602.4 4.9 convolution_convert_fusion.1
  608.9 7.5 convert_reduce_fusion.1
  616.4 14.2 %collective-permute-done.58 = bf16[512,1024]{1,0:T(8,128)(2,1)S(1)} collective-permute-done((bf16[512,1024]{1,0:T(8,128)(2,1)S(1)}, bf16[512,1024]{1,0:T(8,128)(2,1)S(1)}, u32[]{:S(2)}, u32[]{:S(2)}) %collective-permute-start.58) | collective-permute-done | bytes 1048608 | tf_op jit(solution)/shard_map/ppermute | solution.py:202
  632.1 4.1 convolution_convert_fusion.4
  637.6 3.6 convolution_convert_fusion.2
  644.7 21.2 %collective-permute-done.56 = bf16[512,1024]{1,0:T(8,128)(2,1)S(1)} collective-permute-done((bf16[512,1024]{1,0:T(8,128)(2,1)S(1)}, bf16[512,1024]{1,0:T(8,128)(2,1)S(1)}, u32[]{:S(2)}, u32[]{:S(2)}) %collective-permute-start.56) | collective-permute-done | bytes 1048608 | tf_op jit(solution)/shard_map/ppermute | solution.py:202
  677.9 6.8 collective-permute-done.45
  686.8 5.4 collective-permute-start.31
  696.4 3.6 collective-permute-done.54
  705.8 12.1 %attend_back.3 = bf16[1024,768]{1,0:T(8,128)(2,1)} custom-call(s32[1]{0:T(128)} %bitcast.ids_ref, f32[4]{0:T(128)} %multiply_exponential_fusion.slope_ref, bf16[1024,768]{1,0:T(8,128)(2,1)} %add_convert_fusion.1.p_ref, bf16[1024,256]{1,0:T(8,128)(2,1)} %get-tuple-element.18.o_ref, f32[8,1024]{1,0:T(8,128)} %get-tuple-element.21.lse_ref, ...), custom_call_target="tpu_custom_call" | custom-call | flops 24000000000 | bytes 4194304 | tf_op jit(solution)/shard_map/attend_back/pallas_call | solution.py:147
  717.9 3.8 convolution_convert_fusion.10
  723.3 3.8 convolution_convert_fusion.13
  738.3 11.0 %collective-permute-done.48 = bf16[256,1024]{1,0:T(8,128)(2,1)S(1)} collective-permute-done((bf16[256,1024]{1,0:T(8,128)(2,1)}, bf16[256,1024]{1,0:T(8,128)(2,1)S(1)}, u32[]{:S(2)}, u32[]{:S(2)}) %collective-permute-start.48) | collective-permute-done | bytes 524320 | tf_op jit(solution)/shard_map/ppermute | solution.py:193
  761.9 3.6 collective-permute-start.61
  765.5 3.6 collective-permute-start.59
  785.8 111.5 %all-reduce.2.cloned.1.call-done = f32[24,1024]{1,0:T(8,128)} async-done(((f32[24,1024]{1,0:T(8,128)}), f32[24,1024]{1,0:T(8,128)}) %all-reduce.2.cloned.1.call-update) | async-done | bytes 98320 | tf_op jit(solution)/shard_map/psum | solution.py:458
  898.2 29.5 %reduce-scatter.19.cloned.1.call-done = bf16[128,1024]{1,0:T(8,128)(2,1)} async-done(((bf16[512,1024]{1,0:T(8,128)(2,1)}), bf16[128,1024]{1,0:T(8,128)(2,1)}) %reduce-scatter.19.cloned.1.call-update) | async-done | bytes 262160
  (519 shorter events, 213.1 us)
Async XLA Ops:
  7.2 76.6 %all-gather.7.cloned.1.call-start = ((), (), s32[]{:S(2)}) async-start(), calls=%async_computation.6 | async-start | bytes 1310720 | tf_op jit(solution)/shard_map/all_gather | solution.py:197
  10.0 37.2 %collective-permute-start = (bf16[256,1024]{1,0:T(8,128)(2,1)}, bf16[256,1024]{1,0:T(8,128)(2,1)S(1)}, u32[]{:S(2)}, u32[]{:S(2)}) collective-permute-start(bf16[256,1024]{1,0:T(8,128)(2,1)} %param.14), channel_id=1, source_target_pairs={{0,0},{1,4},{2,8},{3,12},{4,1},{5,5},{6,9},{7,13},{8,2},{9,6},{10,... | collective-permute-start | bytes 1572872 | tf_op jit(solution)/shard_map/ppermute | solution.py:169
  47.2 133.2 %all-gather.11.cloned.1.call-start = ((), (), s32[]{:S(2)}) async-start(), calls=%async_computation.8 | async-start | bytes 1310720 | tf_op jit(solution)/shard_map/all_gather | solution.py:197
  48.1 36.3 %collective-permute-start.3 = (bf16[256,1024]{1,0:T(8,128)(2,1)S(1)}, bf16[256,1024]{1,0:T(8,128)(2,1)}, u32[]{:S(2)}, u32[]{:S(2)}) collective-permute-start(bf16[256,1024]{1,0:T(8,128)(2,1)S(1)} %fusion.23), channel_id=1, source_target_pairs={{0,4},{4,0},{1,5},{5,1},{2,6},{6,2},{3,7},{7,3},{8,12},{12,8},{9,1... | collective-permute-start | bytes 1572872 | tf_op jit(solution)/shard_map/ppermute | solution.py:185
  83.7 24.2 %collective-permute-start.6 = (bf16[512,1024]{0,1:T(8,128)(2,1)}, bf16[512,1024]{0,1:T(8,128)(2,1)S(1)}, u32[]{:S(2)}, u32[]{:S(2)}) collective-permute-start(bf16[512,1024]{0,1:T(8,128)(2,1)} %all-gather.7.cloned.1.call-done), channel_id=1, source_target_pairs={{0,16},{16,0},{1,17},{17,1},{2,18},{18,2},{3,19},{19,3},{4,20},{20... | collective-permute-start | bytes 3145736 | tf_op jit(solution)/shard_map/ppermute | solution.py:198
  86.5 21.5 %collective-permute-start.4 = (bf16[512,1024]{1,0:T(8,128)(2,1)}, bf16[512,1024]{1,0:T(8,128)(2,1)}, u32[]{:S(2)}, u32[]{:S(2)}) collective-permute-start(bf16[512,1024]{1,0:T(8,128)(2,1)} %pad_maximum_fusion.10), channel_id=1, source_target_pairs={{0,8},{8,0},{1,9},{9,1},{2,10},{10,2},{3,11},{11,3},{4,12},{12,4},... | collective-permute-start | bytes 3145736 | tf_op jit(solution)/shard_map/ppermute | solution.py:186
  132.3 79.1 %all-gather.9.cloned.1.call-start = ((), (), s32[]{:S(2)}) async-start(), calls=%async_computation.7 | async-start | bytes 1310720 | tf_op jit(solution)/shard_map/all_gather | solution.py:197
  136.1 26.6 %collective-permute-start.8 = (bf16[256,1024]{1,0:T(8,128)(2,1)S(1)}, bf16[256,1024]{1,0:T(8,128)(2,1)S(1)}, u32[]{:S(2)}, u32[]{:S(2)}) collective-permute-start(bf16[256,1024]{1,0:T(8,128)(2,1)S(1)} %slice.711), channel_id=1, source_target_pairs={{0,4},{4,0},{1,5},{5,1},{2,6},{6,2},{3,7},{7,3},{8,12},{12,8},{9,1... | collective-permute-start | bytes 1572872 | tf_op jit(solution)/shard_map/ppermute | solution.py:193
  153.3 137.5 %all-gather.13.cloned.1.call-start = ((), (), s32[]{:S(2)}) async-start(), calls=%async_computation.9 | async-start | bytes 1310720 | tf_op jit(solution)/shard_map/all_gather | solution.py:197
  165.4 47.4 %collective-permute-start.9 = (bf16[256,1024]{1,0:T(8,128)(2,1)S(1)}, bf16[256,1024]{1,0:T(8,128)(2,1)S(1)}, u32[]{:S(2)}, u32[]{:S(2)}) collective-permute-start(bf16[256,1024]{1,0:T(8,128)(2,1)S(1)} %add_convert_fusion.10), channel_id=1, source_target_pairs={{0,4},{4,0},{1,5},{5,1},{2,6},{6,2},{3,7},{7,3},{8,12},{12,8},{9,1... | collective-permute-start | bytes 1572872 | tf_op jit(solution)/shard_map/ppermute | solution.py:185
  180.3 32.9 %collective-permute-start.14 = (bf16[512,1024]{0,1:T(8,128)(2,1)}, bf16[512,1024]{0,1:T(8,128)(2,1)}, u32[]{:S(2)}, u32[]{:S(2)}) collective-permute-start(bf16[512,1024]{0,1:T(8,128)(2,1)} %all-gather.11.cloned.1.call-done), channel_id=1, source_target_pairs={{0,16},{16,0},{1,17},{17,1},{2,18},{18,2},{3,19},{19,3},{4,20},{20... | collective-permute-start | bytes 3145736 | tf_op jit(solution)/shard_map/ppermute | solution.py:198
  211.4 24.6 %collective-permute-start.12 = (bf16[512,1024]{1,0:T(8,128)(2,1)}, bf16[512,1024]{1,0:T(8,128)(2,1)S(1)}, u32[]{:S(2)}, u32[]{:S(2)}) collective-permute-start(bf16[512,1024]{1,0:T(8,128)(2,1)} %all-gather.9.cloned.1.call-done), channel_id=1, source_target_pairs={{0,16},{16,0},{1,17},{17,1},{2,18},{18,2},{3,19},{19,3},{4,20},{20... | collective-permute-start | bytes 3145736 | tf_op jit(solution)/shard_map/ppermute | solution.py:198
  212.9 23.2 %collective-permute-start.10 = (bf16[512,1024]{1,0:T(8,128)(2,1)S(1)}, bf16[512,1024]{1,0:T(8,128)(2,1)S(1)}, u32[]{:S(2)}, u32[]{:S(2)}) collective-permute-start(bf16[512,1024]{1,0:T(8,128)(2,1)S(1)} %pad_maximum_fusion.11), channel_id=1, source_target_pairs={{0,8},{8,0},{1,9},{9,1},{2,10},{10,2},{3,11},{11,3},{4,12},{12,4},... | collective-permute-start | bytes 3145736 | tf_op jit(solution)/shard_map/ppermute | solution.py:186
  245.9 18.6 %collective-permute-start.16 = (bf16[256,1024]{1,0:T(8,128)(2,1)S(1)}, bf16[256,1024]{1,0:T(8,128)(2,1)S(1)}, u32[]{:S(2)}, u32[]{:S(2)}) collective-permute-start(bf16[256,1024]{1,0:T(8,128)(2,1)S(1)} %slice.710), channel_id=1, source_target_pairs={{0,4},{4,0},{1,5},{5,1},{2,6},{6,2},{3,7},{7,3},{8,12},{12,8},{9,1... | collective-permute-start | bytes 1572872 | tf_op jit(solution)/shard_map/ppermute | solution.py:193
  249.1 148.0 %all-gather.17.cloned.1.call-start = ((), (), s32[]{:S(2)}) async-start(), calls=%async_computation.11 | async-start | bytes 1310720 | tf_op jit(solution)/shard_map/all_gather | solution.py:197
  266.6 24.9 %collective-permute-start.17 = (bf16[256,1024]{1,0:T(8,128)(2,1)S(1)}, bf16[256,1024]{1,0:T(8,128)(2,1)S(1)}, u32[]{:S(2)}, u32[]{:S(2)}) collective-permute-start(bf16[256,1024]{1,0:T(8,128)(2,1)S(1)} %add_convert_fusion.9), channel_id=1, source_target_pairs={{0,4},{4,0},{1,5},{5,1},{2,6},{6,2},{3,7},{7,3},{8,12},{12,8},{9,1... | collective-permute-start | bytes 1572872 | tf_op jit(solution)/shard_map/ppermute | solution.py:185
  290.8 24.2 %collective-permute-start.20 = (bf16[512,1024]{0,1:T(8,128)(2,1)}, bf16[512,1024]{0,1:T(8,128)(2,1)S(1)}, u32[]{:S(2)}, u32[]{:S(2)}) collective-permute-start(bf16[512,1024]{0,1:T(8,128)(2,1)} %all-gather.13.cloned.1.call-done), channel_id=1, source_target_pairs={{0,16},{16,0},{1,17},{17,1},{2,18},{18,2},{3,19},{19,3},{4,20},{20... | collective-permute-start | bytes 3145736 | tf_op jit(solution)/shard_map/ppermute | solution.py:198
  291.5 23.5 %collective-permute-start.18 = (bf16[512,1024]{1,0:T(8,128)(2,1)S(1)}, bf16[512,1024]{1,0:T(8,128)(2,1)S(1)}, u32[]{:S(2)}, u32[]{:S(2)}) collective-permute-start(bf16[512,1024]{1,0:T(8,128)(2,1)S(1)} %pad_maximum_fusion.12), channel_id=1, source_target_pairs={{0,8},{8,0},{1,9},{9,1},{2,10},{10,2},{3,11},{11,3},{4,12},{12,4},... | collective-permute-start | bytes 3145736 | tf_op jit(solution)/shard_map/ppermute | solution.py:186
  337.8 91.8 %all-gather.15.cloned.1.call-start = ((), (), s32[]{:S(2)}) async-start(), calls=%async_computation.10 | async-start | bytes 1310720 | tf_op jit(solution)/shard_map/all_gather | solution.py:197
  342.4 26.0 %collective-permute-start.22 = (bf16[256,1024]{1,0:T(8,128)(2,1)S(1)}, bf16[256,1024]{1,0:T(8,128)(2,1)S(1)}, u32[]{:S(2)}, u32[]{:S(2)}) collective-permute-start(bf16[256,1024]{1,0:T(8,128)(2,1)S(1)} %slice.709), channel_id=1, source_target_pairs={{0,4},{4,0},{1,5},{5,1},{2,6},{6,2},{3,7},{7,3},{8,12},{12,8},{9,1... | collective-permute-start | bytes 1572872 | tf_op jit(solution)/shard_map/ppermute | solution.py:193
  357.3 37.1 %collective-permute-start.32 = (bf16[256,1024]{1,0:T(8,128)(2,1)}, bf16[256,1024]{1,0:T(8,128)(2,1)S(1)}, u32[]{:S(2)}, u32[]{:S(2)}) collective-permute-start(bf16[256,1024]{1,0:T(8,128)(2,1)} %param.27), channel_id=1, source_target_pairs={{0,0},{1,4},{2,8},{3,12},{4,1},{5,5},{6,9},{7,13},{8,2},{9,6},{10,... | collective-permute-start | bytes 1572872 | tf_op jit(solution)/shard_map/ppermute | solution.py:169
  359.7 333.1 %reduce-scatter.21.cloned.1.call-start = ((), (), s32[]{:S(2)}) async-start(), calls=%async_computation.18 | async-start | bytes 1310720
  371.1 60.0 %collective-permute-start.23 = (bf16[256,1024]{1,0:T(8,128)(2,1)}, bf16[256,1024]{1,0:T(8,128)(2,1)}, u32[]{:S(2)}, u32[]{:S(2)}) collective-permute-start(bf16[256,1024]{1,0:T(8,128)(2,1)} %add_convert_fusion.8), channel_id=1, source_target_pairs={{0,4},{4,0},{1,5},{5,1},{2,6},{6,2},{3,7},{7,3},{8,12},{12,8},{9,1... | collective-permute-start | bytes 1572872 | tf_op jit(solution)/shard_map/ppermute | solution.py:185
  397.1 36.8 %collective-permute-start.28 = (bf16[512,1024]{0,1:T(8,128)(2,1)}, bf16[512,1024]{0,1:T(8,128)(2,1)}, u32[]{:S(2)}, u32[]{:S(2)}) collective-permute-start(bf16[512,1024]{0,1:T(8,128)(2,1)} %all-gather.17.cloned.1.call-done), channel_id=1, source_target_pairs={{0,16},{16,0},{1,17},{17,1},{2,18},{18,2},{3,19},{19,3},{4,20},{20... | collective-permute-start | bytes 3145736 | tf_op jit(solution)/shard_map/ppermute | solution.py:198
  399.7 32.8 %collective-permute-start.33 = (bf16[256,1024]{1,0:T(8,128)(2,1)S(1)}, bf16[256,1024]{1,0:T(8,128)(2,1)S(1)}, u32[]{:S(2)}, u32[]{:S(2)}) collective-permute-start(bf16[256,1024]{1,0:T(8,128)(2,1)S(1)} %get-tuple-element.107), channel_id=1, source_target_pairs={{0,4},{4,0},{1,5},{5,1},{2,6},{6,2},{3,7},{7,3},{8,12},{12,8},{9,1... | collective-permute-start | bytes 1572872 | tf_op jit(solution)/shard_map/ppermute | solution.py:185
  429.6 24.6 %collective-permute-start.26 = (bf16[512,1024]{1,0:T(8,128)(2,1)}, bf16[512,1024]{1,0:T(8,128)(2,1)S(1)}, u32[]{:S(2)}, u32[]{:S(2)}) collective-permute-start(bf16[512,1024]{1,0:T(8,128)(2,1)} %all-gather.15.cloned.1.call-done), channel_id=1, source_target_pairs={{0,16},{16,0},{1,17},{17,1},{2,18},{18,2},{3,19},{19,3},{4,20},{20... | collective-permute-start | bytes 3145736 | tf_op jit(solution)/shard_map/ppermute | solution.py:198
  432.4 21.9 %collective-permute-start.24 = (bf16[512,1024]{1,0:T(8,128)(2,1)S(1)}, bf16[512,1024]{1,0:T(8,128)(2,1)S(1)}, u32[]{:S(2)}, u32[]{:S(2)}) collective-permute-start(bf16[512,1024]{1,0:T(8,128)(2,1)S(1)} %pad_maximum_fusion.13), channel_id=1, source_target_pairs={{0,8},{8,0},{1,9},{9,1},{2,10},{10,2},{3,11},{11,3},{4,12},{12,4},... | collective-permute-start | bytes 3145736 | tf_op jit(solution)/shard_map/ppermute | solution.py:186
  432.6 25.7 %collective-permute-start.34 = (bf16[512,1024]{1,0:T(8,128)(2,1)S(1)}, bf16[512,1024]{1,0:T(8,128)(2,1)S(1)}, u32[]{:S(2)}, u32[]{:S(2)}) collective-permute-start(bf16[512,1024]{1,0:T(8,128)(2,1)S(1)} %pad_maximum_fusion.14), channel_id=1, source_target_pairs={{0,8},{8,0},{1,9},{9,1},{2,10},{10,2},{3,11},{11,3},{4,12},{12,4},... | collective-permute-start | bytes 3145736 | tf_op jit(solution)/shard_map/ppermute | solution.py:186
  474.0 22.9 %collective-permute-start.30 = (bf16[256,1024]{1,0:T(8,128)(2,1)S(1)}, bf16[256,1024]{1,0:T(8,128)(2,1)S(1)}, u32[]{:S(2)}, u32[]{:S(2)}) collective-permute-start(bf16[256,1024]{1,0:T(8,128)(2,1)S(1)} %slice.708), channel_id=1, source_target_pairs={{0,4},{4,0},{1,5},{5,1},{2,6},{6,2},{3,7},{7,3},{8,12},{12,8},{9,1... | collective-permute-start | bytes 1572872 | tf_op jit(solution)/shard_map/ppermute | solution.py:193
  538.4 25.3 %collective-permute-start.52 = (bf16[512,1024]{0,1:T(8,128)(2,1)S(1)}, bf16[512,1024]{0,1:T(8,128)(2,1)S(1)}, u32[]{:S(2)}, u32[]{:S(2)}) collective-permute-start(bf16[512,1024]{0,1:T(8,128)(2,1)S(1)} %pad_maximum_fusion.8), channel_id=1, source_target_pairs={{0,16},{16,0},{1,17},{17,1},{2,18},{18,2},{3,19},{19,3},{4,20},{20... | collective-permute-start | bytes 3145736 | tf_op jit(solution)/shard_map/ppermute | solution.py:202
  541.2 26.2 %collective-permute-start.40 = (bf16[256,1024]{1,0:T(8,128)(2,1)}, bf16[256,1024]{1,0:T(8,128)(2,1)}, u32[]{:S(2)}, u32[]{:S(2)}) collective-permute-start(bf16[256,1024]{1,0:T(8,128)(2,1)} %slice.706), channel_id=1, source_target_pairs={{0,4},{4,0},{1,5},{5,1},{2,6},{6,2},{3,7},{7,3},{8,12},{12,8},{9,1... | collective-permute-start | bytes 1572872 | tf_op jit(solution)/shard_map/ppermute | solution.py:193
  567.4 194.5 %reduce-scatter.17.cloned.1.call-start = ((), (), s32[]{:S(2)}) async-start(), calls=%async_computation.16 | async-start | bytes 1310720 | tf_op jit(solution)/shard_map/reduce_scatter | solution.py:204
  576.6 24.1 %collective-permute-start.60 = (bf16[512,1024]{1,0:T(8,128)(2,1)S(1)}, bf16[512,1024]{1,0:T(8,128)(2,1)S(1)}, u32[]{:S(2)}, u32[]{:S(2)}) collective-permute-start(bf16[512,1024]{1,0:T(8,128)(2,1)S(1)} %slice.557), channel_id=1, source_target_pairs={{0,16},{16,0},{1,17},{17,1},{2,18},{18,2},{3,19},{19,3},{4,20},{20... | collective-permute-start | bytes 3145736 | tf_op jit(solution)/shard_map/ppermute | solution.py:202
  585.7 16.7 %collective-permute-start.42 = (bf16[512,1024]{1,0:T(8,128)(2,1)S(1)}, bf16[512,1024]{1,0:T(8,128)(2,1)S(1)}, u32[]{:S(2)}, u32[]{:S(2)}) collective-permute-start(bf16[512,1024]{1,0:T(8,128)(2,1)S(1)} %pad_maximum_fusion.16), channel_id=1, source_target_pairs={{0,8},{8,0},{1,9},{9,1},{2,10},{10,2},{3,11},{11,3},{4,12},{12,4},... | collective-permute-start | bytes 3145736 | tf_op jit(solution)/shard_map/ppermute | solution.py:186
  602.1 163.4 %reduce-scatter.15.cloned.1.call-start = ((), (), s32[]{:S(2)}) async-start(), calls=%async_computation.15 | async-start | bytes 1310720 | tf_op jit(solution)/shard_map/reduce_scatter | solution.py:204
  607.4 23.3 %collective-permute-start.58 = (bf16[512,1024]{1,0:T(8,128)(2,1)S(1)}, bf16[512,1024]{1,0:T(8,128)(2,1)S(1)}, u32[]{:S(2)}, u32[]{:S(2)}) collective-permute-start(bf16[512,1024]{1,0:T(8,128)(2,1)S(1)} %slice.555), channel_id=1, source_target_pairs={{0,16},{16,0},{1,17},{17,1},{2,18},{18,2},{3,19},{19,3},{4,20},{20... | collective-permute-start | bytes 3145736 | tf_op jit(solution)/shard_map/ppermute | solution.py:202
  632.1 137.0 %reduce-scatter.13.cloned.1.call-start = ((), (), s32[]{:S(2)}) async-start(), calls=%async_computation.14 | async-start | bytes 1310720 | tf_op jit(solution)/shard_map/reduce_scatter | solution.py:204
  641.3 24.5 %collective-permute-start.56 = (bf16[512,1024]{1,0:T(8,128)(2,1)S(1)}, bf16[512,1024]{1,0:T(8,128)(2,1)S(1)}, u32[]{:S(2)}, u32[]{:S(2)}) collective-permute-start(bf16[512,1024]{1,0:T(8,128)(2,1)S(1)} %slice.552), channel_id=1, source_target_pairs={{0,16},{16,0},{1,17},{17,1},{2,18},{18,2},{3,19},{19,3},{4,20},{20... | collective-permute-start | bytes 3145736 | tf_op jit(solution)/shard_map/ppermute | solution.py:202
  644.0 23.3 %collective-permute-start.44 = (bf16[256,1024]{1,0:T(8,128)(2,1)}, bf16[256,1024]{1,0:T(8,128)(2,1)}, u32[]{:S(2)}, u32[]{:S(2)}) collective-permute-start(bf16[256,1024]{1,0:T(8,128)(2,1)} %slice.705), channel_id=1, source_target_pairs={{0,4},{4,0},{1,5},{5,1},{2,6},{6,2},{3,7},{7,3},{8,12},{12,8},{9,1... | collective-permute-start | bytes 1572872 | tf_op jit(solution)/shard_map/ppermute | solution.py:193
  667.3 107.0 %reduce-scatter.11.cloned.1.call-start = ((), (), s32[]{:S(2)}) async-start(), calls=%async_computation.13 | async-start | bytes 1310720 | tf_op jit(solution)/shard_map/reduce_scatter | solution.py:204
  676.4 23.6 %collective-permute-start.54 = (bf16[512,1024]{1,0:T(8,128)(2,1)}, bf16[512,1024]{1,0:T(8,128)(2,1)}, u32[]{:S(2)}, u32[]{:S(2)}) collective-permute-start(bf16[512,1024]{1,0:T(8,128)(2,1)} %slice.550), channel_id=1, source_target_pairs={{0,16},{16,0},{1,17},{17,1},{2,18},{18,2},{3,19},{19,3},{4,20},{20... | collective-permute-start | bytes 3145736 | tf_op jit(solution)/shard_map/ppermute | solution.py:202
  685.9 17.0 %collective-permute-start.46 = (bf16[512,1024]{1,0:T(8,128)(2,1)}, bf16[512,1024]{1,0:T(8,128)(2,1)}, u32[]{:S(2)}, u32[]{:S(2)}) collective-permute-start(bf16[512,1024]{1,0:T(8,128)(2,1)} %pad_maximum_fusion.17), channel_id=1, source_target_pairs={{0,8},{8,0},{1,9},{9,1},{2,10},{10,2},{3,11},{11,3},{4,12},{12,4},... | collective-permute-start | bytes 3145736 | tf_op jit(solution)/shard_map/ppermute | solution.py:186
  686.8 82.3 %collective-permute-start.31 = (bf16[256,1024]{1,0:T(8,128)(2,1)}, bf16[256,1024]{1,0:T(8,128)(2,1)}, u32[]{:S(2)}, u32[]{:S(2)}) collective-permute-start(bf16[256,1024]{1,0:T(8,128)(2,1)} %maximum_select_fusion.1), channel_id=1, source_target_pairs={{0,0},{1,4},{2,8},{3,12},{4,1},{5,5},{6,9},{7,13},{8,2},{9,6},{10,... | collective-permute-start | bytes 1572872 | tf_op jit(solution)/shard_map/ppermute | solution.py:169
  694.6 78.1 %collective-permute-start.53 = (bf16[128,1024]{0,1:T(8,128)(2,1)}, bf16[128,1024]{0,1:T(8,128)(2,1)S(1)}, u32[]{:S(2)}, u32[]{:S(2)}) collective-permute-start(bf16[128,1024]{0,1:T(8,128)(2,1)} %copy.68), channel_id=1, source_target_pairs={{0,0},{1,4},{2,8},{3,12},{4,1},{5,5},{6,9},{7,13},{8,2},{9,6},{10,... | collective-permute-start | bytes 786440 | tf_op jit(solution)/shard_map/ppermute | solution.py:169
  702.6 194.6 %all-reduce.2.cloned.1.call-start = ((), (), s32[]{:S(2)}) async-start(), calls=%async_computation.12 | async-start | bytes 196608 | tf_op jit(solution)/shard_map/psum | solution.py:458
  730.8 26.0 %collective-permute-start.50 = (bf16[512,1024]{0,1:T(8,128)(2,1)}, bf16[512,1024]{0,1:T(8,128)(2,1)}, u32[]{:S(2)}, u32[]{:S(2)}) collective-permute-start(bf16[512,1024]{0,1:T(8,128)(2,1)} %pad_maximum_fusion.9), channel_id=1, source_target_pairs={{0,16},{16,0},{1,17},{17,1},{2,18},{18,2},{3,19},{19,3},{4,20},{20... | collective-permute-start | bytes 3145736 | tf_op jit(solution)/shard_map/ppermute | solution.py:202
  753.5 174.3 %reduce-scatter.19.cloned.1.call-start = ((), (), s32[]{:S(2)}) async-start(), calls=%async_computation.17 | async-start | bytes 1310720
  785.0 146.5 %collective-permute-start.49 = (bf16[256,1024]{1,0:T(8,128)(2,1)S(1)}, bf16[256,1024]{1,0:T(8,128)(2,1)S(1)}, u32[]{:S(2)}, u32[]{:S(2)}) collective-permute-start(bf16[256,1024]{1,0:T(8,128)(2,1)S(1)} %maximum_select_fusion.3), channel_id=1, source_target_pairs={{0,0},{1,4},{2,8},{3,12},{4,1},{5,5},{6,9},{7,13},{8,2},{9,6},{10,... | collective-permute-start | bytes 1572872 | tf_op jit(solution)/shard_map/ppermute | solution.py:169
  (123 other events, 1609.9 us)
Sparse Core Ops, SparseCore 0:
  47.3 36.4 all-gather.6
  132.4 47.8 all-gather.10
  182.5 28.8 all-gather.8
  249.2 41.4 all-gather.12
  337.9 59.1 all-gather.16
  399.1 30.4 all-gather.14
  567.5 27.2 reduce-scatter.20
  602.2 26.3 reduce-scatter.16
  632.2 26.3 reduce-scatter.14
  667.4 26.2 reduce-scatter.12
  702.8 30.1 reduce-scatter.10
  753.6 143.6 all-reduce.1
  899.6 28.1 reduce-scatter.18
